TPU v7x, 32 devices: a whole 2x2x4 slice. The times are simulated.
32 devices in a mesh: dp: 2 (over x), blk: 4 (over y, core), ulysses: 4 (over z).
Axes of the slice: x: 2, y: 2, z: 4, core: 2. Of those that a mesh axis runs over, the one named last changes fastest.
Arguments:
- tokens: bfloat16 [2, 2048, 1024], P('dp', ('blk', 'ulysses')), may hold values from -20 to 20
- query_weight: bfloat16 [1024, 1024], P(('dp', 'blk'), 'ulysses')
- key_weight: bfloat16 [1024, 1024], P(('dp', 'blk'), 'ulysses')
- value_weight: bfloat16 [1024, 1024], P(('dp', 'blk'), 'ulysses'), may hold values from -0.1875 to 0.1875
- out_weight: bfloat16 [1024, 1024], P('ulysses', ('dp', 'blk'))
- query_bias: bfloat16 [16, 64], P('ulysses', ('dp', 'blk')), may hold values from -4 to 4
- value_bias: bfloat16 [16, 64], P('ulysses', ('dp', 'blk'))
- out_bias: bfloat16 [1024], P(('dp', 'blk')), may hold values from -4 to 4
- norm1_gain: bfloat16 [1024], P(('dp', 'blk')), may hold values from 0.5 to 1.5
- norm1_shift: bfloat16 [1024], P(('dp', 'blk')), may hold values from -4 to 4
- inner_weight: bfloat16 [1024, 4096], P(('dp', 'blk'), 'ulysses'), may hold values from -0.1875 to 0.1875
- inner_bias: bfloat16 [64, 64], P('ulysses', ('dp', 'blk')), may hold values from -4 to 4
- outer_weight: bfloat16 [4096, 1024], P('ulysses', ('dp', 'blk')), may hold values from -0.09375 to 0.09375
- outer_bias: bfloat16 [1024], P(('dp', 'blk')), may hold values from -4 to 4
- norm2_gain: bfloat16 [1024], P(('dp', 'blk')), may hold values from 0.5 to 1.5
- norm2_shift: bfloat16 [1024], P(('dp', 'blk')), may hold values from -4 to 4
- out_grad: bfloat16 [2, 2048, 1024], P('dp', ('blk', 'ulysses')), may hold values from -6 to 6
Outputs:
- block_out: bfloat16 [2, 2048, 1024], P('dp', ('blk', 'ulysses'))
- tokens_grad: bfloat16 [2, 2048, 1024], P('dp', ('blk', 'ulysses'))
- query_weight_grad: float32 [1024, 1024], P(('dp', 'blk'), 'ulysses')
- key_weight_grad: float32 [1024, 1024], P(('dp', 'blk'), 'ulysses')
- value_weight_grad: float32 [1024, 1024], P(('dp', 'blk'), 'ulysses')
- out_weight_grad: float32 [1024, 1024], P('ulysses', ('dp', 'blk'))
- query_bias_grad: float32 [16, 64], P('ulysses', ('dp', 'blk'))
- value_bias_grad: float32 [16, 64], P('ulysses', ('dp', 'blk'))
- out_bias_grad: float32 [1024], P(('dp', 'blk'))
- norm1_gain_grad: float32 [1024], P(('dp', 'blk'))
- norm1_shift_grad: float32 [1024], P(('dp', 'blk'))
- inner_weight_grad: float32 [1024, 4096], P(('dp', 'blk'), 'ulysses')
- inner_bias_grad: float32 [64, 64], P('ulysses', ('dp', 'blk'))
- outer_weight_grad: float32 [4096, 1024], P('ulysses', ('dp', 'blk'))
- outer_bias_grad: float32 [1024], P(('dp', 'blk'))
- norm2_gain_grad: float32 [1024], P(('dp', 'blk'))
- norm2_shift_grad: float32 [1024], P(('dp', 'blk'))
All inputs are finite; a program needn't handle non-finite values.
Results may differ from a plain program's by a relative error of at most 0.035.
Values may be sent and summed in bfloat16 or wider, within the bound.
A program may use at most 128 MiB of HBM per device.

v0:
```python
import math

import jax
import jax.numpy as jnp
from jax import lax
from jax.sharding import PartitionSpec as P

DH = 64


EPSILON = 1e-05


def gelu_parts(pre):
    cdf = 0.5 * (1.0 + lax.erf(pre * 0.7071067811865476))
    dens = jnp.exp(-0.5 * pre * pre) * 0.3989422804014327
    return (pre * cdf, cdf + pre * dens)


def norm_forward(resid, gain, shift):
    centre = resid - jnp.mean(resid, axis=-1, keepdims=True)
    rstd = lax.rsqrt(jnp.mean(centre * centre, axis=-1, keepdims=True) + EPSILON)
    unit = centre * rstd
    return (unit * gain + shift, unit, rstd)


def norm_backward(grad, unit, rstd, gain):
    scaled = grad * gain
    inner = (
        scaled
        - jnp.mean(scaled, axis=-1, keepdims=True)
        - unit * jnp.mean(scaled * unit, axis=-1, keepdims=True)
    )
    return (rstd * inner, jnp.sum(grad * unit, axis=0), jnp.sum(grad, axis=0))


def mat(left, right):
    return jnp.dot(left, right, preferred_element_type=jnp.float32)


def block_terms(sources, weights, extras, count, tok_rows):
    rows_each = tok_rows + extras.shape[0]
    blocks = count // rows_each
    total = None
    for source, weight in zip(sources, weights):
        term = jnp.einsum("te,de->td", source, weight, preferred_element_type=jnp.float32)
        total = term if total is None else total + term
    filler = jnp.broadcast_to(extras[None], (blocks,) + extras.shape)
    joined = jnp.concatenate([total.reshape(blocks, tok_rows, -1), filler], axis=1)
    return joined.reshape(count, -1)


def attend_forward(q_heads, k_heads, v_heads, heads_dev):
    rows, head_width = q_heads.shape
    scale = DH ** (-0.5)
    q_three = q_heads.reshape(rows, heads_dev, DH)

    def fold(carry, piece, start):
        k_piece, v_piece = piece
        count = k_piece.shape[0]
        size = math.gcd(count, 512)
        steps = count // size
        k_split = k_piece.reshape(steps, size, heads_dev, DH)
        v_split = v_piece.reshape(steps, size, heads_dev, DH)

        def step(state, blocks):
            best, total, accum = state
            k_block, v_block = blocks
            scores = (
                jnp.einsum("qhd,khd->hqk", q_three, k_block, preferred_element_type=jnp.float32)
                * scale
            )
            new_best = jnp.maximum(best, jnp.max(scores, axis=-1))
            fade = jnp.exp(best - new_best)
            weights = jnp.exp(scores - new_best[:, :, None])
            total = total * fade + jnp.sum(weights, axis=-1)
            update = jnp.einsum("hqk,khd->qhd", weights, v_block.astype(jnp.float32))
            accum = accum.reshape(rows, heads_dev, DH) * fade.T[:, :, None] + update
            return ((new_best, total, accum.reshape(rows, head_width)), None)

        state, unused = lax.scan(step, carry, (k_split, v_split))
        return state

    start_state = (
        jnp.full((heads_dev, rows), -jnp.inf, jnp.float32),
        jnp.zeros((heads_dev, rows), jnp.float32),
        jnp.zeros((rows, head_width), jnp.float32),
    )
    best, total, accum = fold(
        start_state,
        (
            lax.all_gather(k_heads, "blk", axis=0, tiled=True),
            lax.all_gather(v_heads, "blk", axis=0, tiled=True),
        ),
        jnp.int32(0),
    )
    attended = (accum.reshape(rows, heads_dev, DH) / total.T[:, :, None]).reshape(rows, head_width)
    return (attended.astype(jnp.bfloat16), best + jnp.log(total))


def attend_backward(q_heads, k_heads, v_heads, attended, lse, d_att, heads_dev):
    rows, head_width = q_heads.shape
    scale = DH ** (-0.5)
    q_three = q_heads.reshape(rows, heads_dev, DH)
    do_three = d_att.reshape(rows, heads_dev, DH)
    delta = (
        (d_att.astype(jnp.float32) * attended.astype(jnp.float32))
        .reshape(rows, heads_dev, DH)
        .sum(-1)
        .T
    )
    all_keys = rows * lax.axis_size("blk")

    def fold(carry, piece, start):
        dq_accum, key_accum = carry
        k_piece, v_piece = piece
        count = k_piece.shape[0]
        size = math.gcd(count, 512)
        steps = count // size
        k_split = k_piece.reshape(steps, size, heads_dev, DH)
        v_split = v_piece.reshape(steps, size, heads_dev, DH)

        def step(dq_state, blocks):
            k_block, v_block = blocks
            scores = (
                jnp.einsum("qhd,khd->hqk", q_three, k_block, preferred_element_type=jnp.float32)
                * scale
            )
            weights = jnp.exp(scores - lse[:, :, None])
            weights_round = weights.astype(jnp.bfloat16)
            v_part = jnp.einsum(
                "hqk,qhd->khd", weights_round, do_three, preferred_element_type=jnp.float32
            )
            d_weights = jnp.einsum(
                "qhd,khd->hqk", do_three, v_block, preferred_element_type=jnp.float32
            )
            d_scores = (weights * (d_weights - delta[:, :, None])).astype(jnp.bfloat16)
            q_part = (
                jnp.einsum("hqk,khd->qhd", d_scores, k_block, preferred_element_type=jnp.float32)
                * scale
            )
            k_part = (
                jnp.einsum("hqk,qhd->khd", d_scores, q_three, preferred_element_type=jnp.float32)
                * scale
            )
            dq_state = dq_state + q_part.reshape(rows, head_width)
            both = jnp.stack(
                [k_part.reshape(size, head_width), v_part.reshape(size, head_width)], axis=1
            )
            return (dq_state, both)

        dq_accum, parts = lax.scan(step, dq_accum, (k_split, v_split))
        parts = parts.reshape(count, 2, head_width)
        key_accum = parts
        return (dq_accum, key_accum)

    start_state = (
        jnp.zeros((rows, head_width), jnp.float32),
        jnp.zeros((all_keys, 2, head_width), jnp.float32),
    )
    dq_accum, key_accum = fold(
        start_state,
        (
            lax.all_gather(k_heads, "blk", axis=0, tiled=True),
            lax.all_gather(v_heads, "blk", axis=0, tiled=True),
        ),
        jnp.int32(0),
    )
    owned = lax.psum_scatter(
        key_accum.astype(jnp.bfloat16), "blk", scatter_dimension=0, tiled=True
    ).astype(jnp.float32)
    return (
        dq_accum.astype(jnp.bfloat16),
        owned[:, 0].astype(jnp.bfloat16),
        owned[:, 1].astype(jnp.bfloat16),
    )


def local(
    tokens,
    query_weight,
    key_weight,
    value_weight,
    out_weight,
    query_bias,
    value_bias,
    out_bias,
    norm1_gain,
    norm1_shift,
    inner_weight,
    inner_bias,
    outer_weight,
    outer_bias,
    norm2_gain,
    norm2_shift,
    out_grad,
):
    (
        w_query,
        w_key,
        w_value,
        w_out,
        w_inner,
        w_outer,
        b_query,
        b_value,
        b_inner,
        b_out,
        gain_one,
        shift_one,
        b_outer,
        gain_two,
        shift_two,
    ) = (
        lax.all_gather(query_weight, ("dp", "blk"), axis=0, tiled=True),
        lax.all_gather(key_weight, ("dp", "blk"), axis=0, tiled=True),
        lax.all_gather(value_weight, ("dp", "blk"), axis=0, tiled=True),
        lax.all_gather(out_weight, ("dp", "blk"), axis=1, tiled=True),
        lax.all_gather(inner_weight, ("dp", "blk"), axis=0, tiled=True),
        lax.all_gather(outer_weight, ("dp", "blk"), axis=1, tiled=True),
        lax.all_gather(query_bias, ("dp", "blk"), axis=1, tiled=True),
        lax.all_gather(value_bias, ("dp", "blk"), axis=1, tiled=True),
        lax.all_gather(inner_bias, ("dp", "blk"), axis=1, tiled=True),
        lax.all_gather(out_bias, ("dp", "blk"), axis=0, tiled=True),
        lax.all_gather(norm1_gain, ("dp", "blk"), axis=0, tiled=True),
        lax.all_gather(norm1_shift, ("dp", "blk"), axis=0, tiled=True),
        lax.all_gather(outer_bias, ("dp", "blk"), axis=0, tiled=True),
        lax.all_gather(norm2_gain, ("dp", "blk"), axis=0, tiled=True),
        lax.all_gather(norm2_shift, ("dp", "blk"), axis=0, tiled=True),
    )
    rows_in = tokens[0]
    tok_rows, width = rows_in.shape
    head_width = w_query.shape[1]
    heads_dev = head_width // DH
    rows_all = lax.all_gather(rows_in, "ulysses", axis=0, tiled=True)
    q_heads = (mat(rows_all, w_query) + b_query.reshape(-1).astype(jnp.float32)).astype(
        jnp.bfloat16
    )
    k_heads = mat(rows_all, w_key).astype(jnp.bfloat16)
    v_heads = (mat(rows_all, w_value) + b_value.reshape(-1).astype(jnp.float32)).astype(
        jnp.bfloat16
    )
    attended, lse = attend_forward(q_heads, k_heads, v_heads, heads_dev)
    attn_sum = lax.psum_scatter(
        mat(attended, w_out).astype(jnp.bfloat16), "ulysses", scatter_dimension=0, tiled=True
    ).astype(jnp.float32)
    resid_one = rows_in.astype(jnp.float32) + attn_sum + b_out.astype(jnp.float32)
    normed_one, unit_one, rstd_one = norm_forward(
        resid_one, gain_one.astype(jnp.float32), shift_one.astype(jnp.float32)
    )
    normed_round = normed_one.astype(jnp.bfloat16)
    normed_all = lax.all_gather(normed_round, "ulysses", axis=0, tiled=True)
    pre_act = mat(normed_all, w_inner) + b_inner.reshape(-1).astype(jnp.float32)
    act_full, slope = gelu_parts(pre_act)
    activation = act_full.astype(jnp.bfloat16)
    ffn_sum = lax.psum_scatter(
        mat(activation, w_outer).astype(jnp.bfloat16), "ulysses", scatter_dimension=0, tiled=True
    ).astype(jnp.float32)
    resid_two = normed_one + ffn_sum + b_outer.astype(jnp.float32)
    final, unit_two, rstd_two = norm_forward(
        resid_two, gain_two.astype(jnp.float32), shift_two.astype(jnp.float32)
    )
    block_out = final.astype(jnp.bfloat16)[None]
    d_resid_two, g_gain_two, g_shift_two = norm_backward(
        out_grad[0].astype(jnp.float32), unit_two, rstd_two, gain_two.astype(jnp.float32)
    )
    g_outer_b = jnp.sum(d_resid_two, axis=0)
    d_two_round = d_resid_two.astype(jnp.bfloat16)
    d_two_all = lax.all_gather(d_two_round, "ulysses", axis=0, tiled=True)
    g_outer_w = jnp.einsum("tf,td->fd", activation, d_two_all, preferred_element_type=jnp.float32)
    d_pre = jnp.einsum("td,fd->tf", d_two_all, w_outer, preferred_element_type=jnp.float32) * slope
    d_pre_round = d_pre.astype(jnp.bfloat16)
    g_inner_w = jnp.einsum("td,tf->df", normed_all, d_pre_round, preferred_element_type=jnp.float32)
    g_inner_b = jnp.sum(d_pre, axis=0).reshape(-1, DH)
    extras_two = jnp.stack([g_gain_two, g_shift_two, g_outer_b], axis=0)
    kept_two = lax.psum_scatter(
        block_terms(
            (d_pre_round,),
            (w_inner,),
            extras_two,
            (tok_rows + 3) * lax.axis_size("ulysses"),
            tok_rows,
        ).astype(jnp.bfloat16),
        "ulysses",
        scatter_dimension=0,
        tiled=True,
    ).astype(jnp.float32)
    d_normed = d_resid_two + kept_two[:tok_rows]
    sum_gain_two = kept_two[tok_rows]
    sum_shift_two = kept_two[tok_rows + 1]
    sum_outer_b = kept_two[tok_rows + 2]
    d_resid_one, g_gain_one, g_shift_one = norm_backward(
        d_normed, unit_one, rstd_one, gain_one.astype(jnp.float32)
    )
    g_out_b = jnp.sum(d_resid_one, axis=0)
    d_one_round = d_resid_one.astype(jnp.bfloat16)
    d_one_all = lax.all_gather(d_one_round, "ulysses", axis=0, tiled=True)
    g_out_w = jnp.einsum("te,td->ed", attended, d_one_all, preferred_element_type=jnp.float32)
    d_att = jnp.einsum("td,ed->te", d_one_all, w_out, preferred_element_type=jnp.float32).astype(
        jnp.bfloat16
    )
    dq_heads, dk_heads, dv_heads = attend_backward(
        q_heads, k_heads, v_heads, attended, lse, d_att, heads_dev
    )
    g_query_w = jnp.einsum("td,te->de", rows_all, dq_heads, preferred_element_type=jnp.float32)
    g_key_w = jnp.einsum("td,te->de", rows_all, dk_heads, preferred_element_type=jnp.float32)
    g_value_w = jnp.einsum("td,te->de", rows_all, dv_heads, preferred_element_type=jnp.float32)
    g_query_b = jnp.sum(dq_heads.astype(jnp.float32), axis=0).reshape(-1, DH)
    g_value_b = jnp.sum(dv_heads.astype(jnp.float32), axis=0).reshape(-1, DH)
    extras_one = jnp.stack([g_gain_one, g_shift_one, g_out_b], axis=0)
    kept_one = lax.psum_scatter(
        block_terms(
            (dq_heads, dk_heads, dv_heads),
            (w_query, w_key, w_value),
            extras_one,
            (tok_rows + 3) * lax.axis_size("ulysses"),
            tok_rows,
        ).astype(jnp.bfloat16),
        "ulysses",
        scatter_dimension=0,
        tiled=True,
    ).astype(jnp.float32)
    tokens_grad = (d_resid_one + kept_one[:tok_rows]).astype(jnp.bfloat16)[None]
    sum_gain_one = kept_one[tok_rows]
    sum_shift_one = kept_one[tok_rows + 1]
    sum_out_b = kept_one[tok_rows + 2]
    reduced = (
        lax.psum_scatter(
            g_query_w.astype(jnp.bfloat16), ("dp", "blk"), scatter_dimension=0, tiled=True
        ).astype(jnp.float32),
        lax.psum_scatter(
            g_key_w.astype(jnp.bfloat16), ("dp", "blk"), scatter_dimension=0, tiled=True
        ).astype(jnp.float32),
        lax.psum_scatter(
            g_value_w.astype(jnp.bfloat16), ("dp", "blk"), scatter_dimension=0, tiled=True
        ).astype(jnp.float32),
        lax.psum_scatter(
            g_out_w.astype(jnp.bfloat16), ("dp", "blk"), scatter_dimension=1, tiled=True
        ).astype(jnp.float32),
        lax.psum_scatter(
            g_inner_w.astype(jnp.bfloat16), ("dp", "blk"), scatter_dimension=0, tiled=True
        ).astype(jnp.float32),
        lax.psum_scatter(
            g_outer_w.astype(jnp.bfloat16), ("dp", "blk"), scatter_dimension=1, tiled=True
        ).astype(jnp.float32),
        lax.psum_scatter(
            g_query_b.astype(jnp.bfloat16), ("dp", "blk"), scatter_dimension=1, tiled=True
        ).astype(jnp.float32),
        lax.psum_scatter(
            g_value_b.astype(jnp.bfloat16), ("dp", "blk"), scatter_dimension=1, tiled=True
        ).astype(jnp.float32),
        lax.psum_scatter(
            g_inner_b.astype(jnp.bfloat16), ("dp", "blk"), scatter_dimension=1, tiled=True
        ).astype(jnp.float32),
        lax.psum_scatter(
            sum_out_b.astype(jnp.bfloat16), ("dp", "blk"), scatter_dimension=0, tiled=True
        ).astype(jnp.float32),
        lax.psum_scatter(
            sum_gain_one.astype(jnp.bfloat16), ("dp", "blk"), scatter_dimension=0, tiled=True
        ).astype(jnp.float32),
        lax.psum_scatter(
            sum_shift_one.astype(jnp.bfloat16), ("dp", "blk"), scatter_dimension=0, tiled=True
        ).astype(jnp.float32),
        lax.psum_scatter(
            sum_outer_b.astype(jnp.bfloat16), ("dp", "blk"), scatter_dimension=0, tiled=True
        ).astype(jnp.float32),
        lax.psum_scatter(
            sum_gain_two.astype(jnp.bfloat16), ("dp", "blk"), scatter_dimension=0, tiled=True
        ).astype(jnp.float32),
        lax.psum_scatter(
            sum_shift_two.astype(jnp.bfloat16), ("dp", "blk"), scatter_dimension=0, tiled=True
        ).astype(jnp.float32),
    )
    return (
        block_out,
        tokens_grad,
        reduced[0],
        reduced[1],
        reduced[2],
        reduced[3],
        reduced[6],
        reduced[7],
        reduced[9],
        reduced[10],
        reduced[11],
        reduced[4],
        reduced[8],
        reduced[5],
        reduced[12],
        reduced[13],
        reduced[14],
    )


def solution(mesh):
    in_specs = (
        P("dp", ("blk", "ulysses"), None),
        P(("dp", "blk"), "ulysses"),
        P(("dp", "blk"), "ulysses"),
        P(("dp", "blk"), "ulysses"),
        P("ulysses", ("dp", "blk")),
        P("ulysses", ("dp", "blk")),
        P("ulysses", ("dp", "blk")),
        P(("dp", "blk")),
        P(("dp", "blk")),
        P(("dp", "blk")),
        P(("dp", "blk"), "ulysses"),
        P("ulysses", ("dp", "blk")),
        P("ulysses", ("dp", "blk")),
        P(("dp", "blk")),
        P(("dp", "blk")),
        P(("dp", "blk")),
        P("dp", ("blk", "ulysses"), None),
    )
    out_specs = (
        P("dp", ("blk", "ulysses"), None),
        P("dp", ("blk", "ulysses"), None),
        P(("dp", "blk"), "ulysses"),
        P(("dp", "blk"), "ulysses"),
        P(("dp", "blk"), "ulysses"),
        P("ulysses", ("dp", "blk")),
        P("ulysses", ("dp", "blk")),
        P("ulysses", ("dp", "blk")),
        P(("dp", "blk")),
        P(("dp", "blk")),
        P(("dp", "blk")),
        P(("dp", "blk"), "ulysses"),
        P("ulysses", ("dp", "blk")),
        P("ulysses", ("dp", "blk")),
        P(("dp", "blk")),
        P(("dp", "blk")),
        P(("dp", "blk")),
    )
    return jax.shard_map(local, mesh=mesh, in_specs=in_specs, out_specs=out_specs, check_vma=False)
```

profile of v0, /device:TPU:0, one launch (start us, length us, event | category | flops | bytes accessed | tf_op | source)
XLA Modules:
  0.0 686.7 jit_solution(14132565026352096235)
XLA Ops:
  8.8 10.6 %all-gather.2 = bf16[8,8,4]{1,2,0:T(4,128)(2,1)S(1)} all-gather(bf16[1,8,4]{1,2,0:T(4,128)(2,1)} %bitcast.292), channel_id=1, replica_groups=mesh['dp'=2,'blk'=4,'ulysses'=4] {'dp','blk'}, dimensions={0}, use_global_device_ids=true | all-gather | bytes 576 | tf_op jit(solution)/shard_map/all_gather | solution.py:222
  19.5 9.7 %all_gather.70 = bf16[1024,256]{1,0:T(8,128)(2,1)S(1)} all-gather(bf16[128,256]{1,0:T(8,128)(2,1)} %param.24), channel_id=1, replica_groups=mesh['dp'=2,'blk'=4,'ulysses'=4] {'dp','blk'}, dimensions={0}, use_global_device_ids=true | all-gather | bytes 589824 | tf_op jit(solution)/shard_map/all_gather | solution.py:217
  29.2 11.9 %all-gather.32.cloned.1.call-done = bf16[1,512,1024]{2,1,0:T(8,128)(2,1)} async-done(((bf16[1,128,1024]{2,1,0:T(8,128)(2,1)}), bf16[1,512,1024]{2,1,0:T(8,128)(2,1)}) %all-gather.32.cloned.1.call-update) | async-done | bytes 1048592 | tf_op jit(solution)/shard_map/all_gather | solution.py:235
  41.2 2.5 fusion.47
  43.7 9.8 %all_gather.66 = bf16[1024,256]{1,0:T(8,128)(2,1)S(1)} all-gather(bf16[128,256]{1,0:T(8,128)(2,1)S(1)} %copy-done.16), channel_id=1, replica_groups=mesh['dp'=2,'blk'=4,'ulysses'=4] {'dp','blk'}, dimensions={0}, use_global_device_ids=true | all-gather | bytes 589824 | tf_op jit(solution)/shard_map/all_gather | solution.py:216
  55.6 10.1 %all-gather.1 = bf16[8,8,4]{1,2,0:T(4,128)(2,1)S(1)} all-gather(bf16[1,8,4]{1,2,0:T(4,128)(2,1)S(1)} %bitcast.293), channel_id=1, replica_groups=mesh['dp'=2,'blk'=4,'ulysses'=4] {'dp','blk'}, dimensions={0}, use_global_device_ids=true | all-gather | bytes 576 | tf_op jit(solution)/shard_map/all_gather | solution.py:221
  65.9 10.2 %all_gather.68 = bf16[1024,256]{1,0:T(8,128)(2,1)S(1)} all-gather(bf16[128,256]{1,0:T(8,128)(2,1)S(1)} %copy-done.17), channel_id=1, replica_groups=mesh['dp'=2,'blk'=4,'ulysses'=4] {'dp','blk'}, dimensions={0}, use_global_device_ids=true | all-gather | bytes 589824 | tf_op jit(solution)/shard_map/all_gather | solution.py:215
  76.0 11.2 %all_gather.73 = bf16[256,1024]{1,0:T(8,128)(2,1)} all-gather(bf16[256,128]{1,0:T(8,128)(2,1)S(1)} %copy-done.18), channel_id=1, replica_groups=mesh['dp'=2,'blk'=4,'ulysses'=4] {'dp','blk'}, dimensions={1}, use_global_device_ids=true | all-gather | bytes 589824 | tf_op jit(solution)/shard_map/all_gather | solution.py:218
  87.8 3.3 reshape.245
  91.1 2.3 copy.93
  93.4 3.3 reshape.244
  96.8 1.2 copy.92
  98.1 13.8 %while.28 = (s32[]{:T(128)}, f32[4,512]{1,0:T(4,128)S(1)}, f32[4,512]{1,0:T(4,128)S(1)}, f32[512,256]{0,1:T(8,128)S(1)}, bf16[4,512,4,64]{1,3,2,0:T(8,128)(2,1)S...) while((s32[]{:T(128)}, f32[4,512]{1,0:T(4,128)S(1)}, ...), condition=%wide.region_3.4_spmd.clone, body=%wide.region_0.3_spmd.clone.sunk | while | flops 276049920 | bytes 14549112 | solution.py:81
  99.6 1.9 fusion.142
  103.0 1.9 fusion.142
  106.5 1.9 fusion.142
  110.0 1.9 fusion.142
  112.7 1.4 convolution_convert_fusion.4
  114.8 7.9 %all-gather.3 = bf16[8,1,128]{2,1,0:T(2,128)(2,1)S(1)} all-gather(bf16[1,1,128]{2,1,0:T(2,128)(2,1)S(1)} %bitcast.294), channel_id=1, replica_groups=mesh['dp'=2,'blk'=4,'ulysses'=4] {'dp','blk'}, dimensions={0}, use_global_device_ids=true | all-gather | bytes 2304 | tf_op jit(solution)/shard_map/all_gather | solution.py:224
  122.8 8.7 %all-gather.4 = bf16[8,1,128]{2,1,0:T(2,128)(2,1)S(1)} all-gather(bf16[1,1,128]{2,1,0:T(2,128)(2,1)S(1)} %bitcast.295), channel_id=1, replica_groups=mesh['dp'=2,'blk'=4,'ulysses'=4] {'dp','blk'}, dimensions={0}, use_global_device_ids=true | all-gather | bytes 2304 | tf_op jit(solution)/shard_map/all_gather | solution.py:225
  131.5 8.0 %all-gather.5 = bf16[8,1,128]{2,1,0:T(2,128)(2,1)S(1)} all-gather(bf16[1,1,128]{2,1,0:T(2,128)(2,1)S(1)} %bitcast.296), channel_id=1, replica_groups=mesh['dp'=2,'blk'=4,'ulysses'=4] {'dp','blk'}, dimensions={0}, use_global_device_ids=true | all-gather | bytes 2304 | tf_op jit(solution)/shard_map/all_gather | solution.py:226
  142.0 1.8 fusion.67
  144.5 9.1 %all_gather.79 = bf16[16,64]{0,1:T(8,128)(2,1)S(1)} all-gather(bf16[16,8]{0,1:T(8,128)(2,1)S(1)} %copy-done.19), channel_id=1, replica_groups=mesh['dp'=2,'blk'=4,'ulysses'=4] {'dp','blk'}, dimensions={1}, use_global_device_ids=true | all-gather | bytes 2304 | tf_op jit(solution)/shard_map/all_gather | solution.py:223
  153.7 18.6 %all-gather.22.cloned.1.call-done = bf16[512,1024]{1,0:T(8,128)(2,1)} async-done(((bf16[128,1024]{1,0:T(8,128)(2,1)}), bf16[512,1024]{1,0:T(8,128)(2,1)}) %all-gather.22.cloned.1.call-update) | async-done | bytes 1048592 | tf_op jit(solution)/shard_map/all_gather | solution.py:252
  172.3 5.0 multiply_convert_fusion.1
  177.2 24.1 %all-gather.26.cloned.1.call-done = bf16[1024,1024]{1,0:T(8,128)(2,1)} async-done(((bf16[1024,128]{1,0:T(8,128)(2,1)}), bf16[1024,1024]{1,0:T(8,128)(2,1)}) %all-gather.26.cloned.1.call-update) | async-done | bytes 2097168 | tf_op jit(solution)/shard_map/all_gather | solution.py:220
  201.3 4.2 convolution_convert_fusion.3
  205.6 8.7 %all-gather.6 = bf16[8,1,128]{2,1,0:T(2,128)(2,1)S(1)} all-gather(bf16[1,1,128]{2,1,0:T(2,128)(2,1)S(1)} %bitcast.297), channel_id=1, replica_groups=mesh['dp'=2,'blk'=4,'ulysses'=4] {'dp','blk'}, dimensions={0}, use_global_device_ids=true | all-gather | bytes 2304 | tf_op jit(solution)/shard_map/all_gather | solution.py:227
  214.4 7.8 %all-gather.7 = bf16[8,1,128]{2,1,0:T(2,128)(2,1)S(1)} all-gather(bf16[1,1,128]{2,1,0:T(2,128)(2,1)S(1)} %bitcast.298), channel_id=1, replica_groups=mesh['dp'=2,'blk'=4,'ulysses'=4] {'dp','blk'}, dimensions={0}, use_global_device_ids=true | all-gather | bytes 2304 | tf_op jit(solution)/shard_map/all_gather | solution.py:228
  222.2 8.7 %all-gather.8 = bf16[8,1,128]{2,1,0:T(2,128)(2,1)S(1)} all-gather(bf16[1,1,128]{2,1,0:T(2,128)(2,1)S(1)} %bitcast.299), channel_id=1, replica_groups=mesh['dp'=2,'blk'=4,'ulysses'=4] {'dp','blk'}, dimensions={0}, use_global_device_ids=true | all-gather | bytes 2304 | tf_op jit(solution)/shard_map/all_gather | solution.py:229
  230.9 2.1 reduce-scatter.25.cloned.1.call-done
  233.0 1.3 fusion.84
  236.0 26.5 %all-gather.28.cloned.1.call-done = bf16[512,1024]{1,0:T(8,128)(2,1)} async-done(((bf16[128,1024]{1,0:T(8,128)(2,1)}), bf16[512,1024]{1,0:T(8,128)(2,1)}) %all-gather.28.cloned.1.call-update) | async-done | bytes 1048592 | tf_op jit(solution)/shard_map/all_gather | solution.py:269
  262.5 4.6 fusion.85
  267.1 1.3 convolution_convert_fusion.2
  268.5 1.3 convert_element_type.287
  271.2 50.9 %all-reduce.15.cloned.1.call-done = bf16[524,1024]{1,0:T(8,128)(2,1)} async-done(((bf16[524,1024]{1,0:T(8,128)(2,1)}), bf16[524,1024]{1,0:T(8,128)(2,1)}) %all-reduce.15.cloned.1.call-update) | async-done | bytes 1073168
  322.1 1.4 multiply_reduce_fusion
  324.7 27.2 %all-gather.30.cloned.1.call-done = bf16[512,1024]{1,0:T(8,128)(2,1)} async-done(((bf16[128,1024]{1,0:T(8,128)(2,1)}), bf16[512,1024]{1,0:T(8,128)(2,1)}) %all-gather.30.cloned.1.call-update) | async-done | bytes 1048592 | tf_op jit(solution)/shard_map/all_gather | solution.py:297
  352.0 1.7 bitcast_reduce_fusion.1
  353.7 25.3 %while.29 = (s32[]{:T(128)}, f32[512,256]{0,1:T(8,128)S(1)}, bf16[4,512,2,256]{3,1,0,2:T(8,128)(2,1)}, bf16[4,512,4,64]{1,3,2,0:T(8,128)(2,1)S(1)}, bf16[512,4,6...) while((s32[]{:T(128)}, f32[512,256]{0,1:T(8,128)S(1)}, ...), condition=%wide.region_20.21_spmd.clone, body=%wide.region_19.20_spmd.clone.sunk | while | flops 680394752 | bytes 26501264 | solution.py:152
  355.3 2.2 multiply_convert_fusion.3
  361.6 2.2 multiply_convert_fusion.3
  367.9 2.2 multiply_convert_fusion.3
  374.2 2.2 multiply_convert_fusion.3
  380.5 2.7 convolution_convert_fusion
  383.2 4.1 copy.117
  388.9 2.7 convolution_convert_fusion.1
  391.7 1.7 convolution_convert_fusion.5
  396.1 13.5 %reduce-scatter.27.cloned.1.call-done = bf16[512,2,256]{2,0,1:T(8,128)(2,1)} async-done(((bf16[2048,2,256]{2,0,1:T(8,128)(2,1)}), bf16[512,2,256]{2,0,1:T(8,128)(2,1)}) %reduce-scatter.27.cloned.1.call-update) | async-done | bytes 524304 | tf_op jit(solution)/shard_map/reduce_scatter | solution.py:169
  409.7 1.4 fusion.45
  412.3 1.9 fusion.79
  415.7 1.5 fusion.73
  417.2 2.3 add_convert_fusion
  419.7 1.3 convert_element_type.297
  424.0 30.1 %reduce-scatter.39.cloned.1.call-done = bf16[128,1024]{1,0:T(8,128)(2,1)} async-done(((bf16[1024,1024]{1,0:T(8,128)(2,1)}), bf16[128,1024]{1,0:T(8,128)(2,1)}) %reduce-scatter.39.cloned.1.call-update) | async-done | bytes 262160
  456.0 42.5 %reduce-scatter.29.cloned.1.call-done = bf16[128,1024]{1,0:T(8,128)(2,1)} async-done(((bf16[1024,1024]{1,0:T(8,128)(2,1)}), bf16[128,1024]{1,0:T(8,128)(2,1)}) %reduce-scatter.29.cloned.1.call-update) | async-done | bytes 262160 | tf_op jit(solution)/shard_map/reduce_scatter | solution.py:340
  498.5 1.8 convert_element_type.321
  500.3 35.3 %reduce-scatter.37.cloned.1.call-done = bf16[128,256]{1,0:T(8,128)(2,1)} async-done(((bf16[1024,256]{1,0:T(8,128)(2,1)}), bf16[128,256]{1,0:T(8,128)(2,1)}) %reduce-scatter.37.cloned.1.call-update) | async-done | bytes 65552
  537.2 35.6 %reduce-scatter.31.cloned.1.call-done = bf16[128,256]{1,0:T(8,128)(2,1)} async-done(((bf16[1024,256]{1,0:T(8,128)(2,1)}), bf16[128,256]{1,0:T(8,128)(2,1)}) %reduce-scatter.31.cloned.1.call-update) | async-done | bytes 65552
  574.7 35.2 %reduce-scatter.35.cloned.1.call-done = bf16[128,256]{1,0:T(8,128)(2,1)} async-done(((bf16[1024,256]{1,0:T(8,128)(2,1)}), bf16[128,256]{1,0:T(8,128)(2,1)}) %reduce-scatter.35.cloned.1.call-update) | async-done | bytes 65552
  611.7 35.5 %reduce-scatter.33.cloned.1.call-done = bf16[128,256]{1,0:T(8,128)(2,1)} async-done(((bf16[1024,256]{1,0:T(8,128)(2,1)}), bf16[128,256]{1,0:T(8,128)(2,1)}) %reduce-scatter.33.cloned.1.call-update) | async-done | bytes 65552
  649.8 22.5 %all-reduce.11 = (bf16[4,64]{1,0:T(4,128)(2,1)S(1)}, bf16[4,64]{1,0:T(4,128)(2,1)S(1)}, bf16[1024]{0:T(1024)(128)(2,1)S(1)}, bf16[1024]{0:T(1024)(128)(2,1)S(1)}...) all-reduce(bf16[4,64]{1,0:T(4,128)(2,1)S(1)} %convert_element_type., ...), channel_id=12, replica_groups=mesh['dp'=2,'blk'=4,'ulysses'=4] {'dp','blk'}, use_global_device_ids=true, to_apply=%region_31.32.clone | all-reduce | flops 7680 | bytes 30720
  677.8 1.7 fusion.70
  (245 shorter events, 60.3 us)
Async XLA Ops:
  8.0 35.7 %copy-start.16 = (bf16[128,256]{1,0:T(8,128)(2,1)S(1)}, bf16[128,256]{1,0:T(8,128)(2,1)}, u32[]{:S(2)}) copy-start(bf16[128,256]{1,0:T(8,128)(2,1)} %param.23) | copy-start | bytes 196612
  8.0 33.1 %all-gather.32.cloned.1.call-start = ((), (), s32[]{:S(2)}) async-start(), calls=%async_computation.20 | async-start | bytes 1310720 | tf_op jit(solution)/shard_map/all_gather | solution.py:235
  8.8 79.0 %all-gather.20.cloned.1.call-start = ((), (), s32[]{:S(2)}) async-start(), calls=%async_computation.10 | async-start | bytes 1310720 | tf_op jit(solution)/shard_map/all_gather | solution.py:93
  29.2 26.2 %copy-start.9 = (bf16[1024,256]{1,0:T(8,128)(2,1)}, bf16[1024,256]{1,0:T(8,128)(2,1)S(1)}, u32[]{:S(2)}) copy-start(bf16[1024,256]{1,0:T(8,128)(2,1)S(1)} %all_gather.70) | copy-start | bytes 1572868
  29.2 26.3 %copy-start.20 = (bf16[4,8]{1,0:T(4,128)(2,1)S(1)}, bf16[4,8]{1,0:T(4,128)(2,1)}, u32[]{:S(2)}) copy-start(bf16[4,8]{1,0:T(4,128)(2,1)} %param.26) | copy-start | bytes 196
  29.2 36.7 %copy-start.17 = (bf16[128,256]{1,0:T(8,128)(2,1)S(1)}, bf16[128,256]{1,0:T(8,128)(2,1)}, u32[]{:S(2)}) copy-start(bf16[128,256]{1,0:T(8,128)(2,1)} %param.22) | copy-start | bytes 196612
  41.1 13.2 %copy-start.1 = (bf16[1,512,1024]{2,1,0:T(8,128)(2,1)S(1)}, bf16[1,512,1024]{2,1,0:T(8,128)(2,1)}, u32[]{:S(2)}) copy-start(bf16[1,512,1024]{2,1,0:T(8,128)(2,1)} %all-gather.32.cloned.1.call-done) | copy-start | bytes 3145732
  43.6 32.4 %copy-start.18 = (bf16[256,128]{1,0:T(8,128)(2,1)S(1)}, bf16[256,128]{1,0:T(8,128)(2,1)}, u32[]{:S(2)}) copy-start(bf16[256,128]{1,0:T(8,128)(2,1)} %param.25) | copy-start | bytes 196612
  43.6 49.8 %all-gather.18.cloned.1.call-start = ((), (), s32[]{:S(2)}) async-start(), calls=%async_computation.9 | async-start | bytes 1310720 | tf_op jit(solution)/shard_map/all_gather | solution.py:92
  53.5 0.8 copy-start.13
  55.5 84.2 %reduce-scatter.23.cloned.1.call-start = ((), (), s32[]{:S(2)}) async-start(), calls=%async_computation.11 | async-start | bytes 1310720 | tf_op jit(solution)/shard_map/reduce_scatter | solution.py:244
  76.0 11.2 %copy-start.14 = (bf16[1024,256]{1,0:T(8,128)(2,1)}, bf16[1024,256]{1,0:T(8,128)(2,1)S(1)}, u32[]{:S(2)}) copy-start(bf16[1024,256]{1,0:T(8,128)(2,1)S(1)} %all_gather.68) | copy-start | bytes 1572868
  98.1 14.7 %copy-start.11 = (bf16[256,1024]{1,0:T(8,128)(2,1)S(1)}, bf16[256,1024]{1,0:T(8,128)(2,1)}, u32[]{:S(2)}) copy-start(bf16[256,1024]{1,0:T(8,128)(2,1)} %all_gather.73) | copy-start | bytes 1572868
  111.9 2.9 copy-start.21
  111.9 10.9 %copy-start.22 = (bf16[128]{0:T(256)(128)(2,1)S(1)}, bf16[128]{0:T(256)(128)(2,1)}, u32[]{:S(2)}) copy-start(bf16[128]{0:T(256)(128)(2,1)} %param.29) | copy-start | bytes 772
  111.9 19.5 %copy-start.23 = (bf16[128]{0:T(256)(128)(2,1)S(1)}, bf16[128]{0:T(256)(128)(2,1)}, u32[]{:S(2)}) copy-start(bf16[128]{0:T(256)(128)(2,1)} %param.30) | copy-start | bytes 772
  111.9 27.8 %copy-start = (bf16[1,128,1024]{2,1,0:T(8,128)(2,1)S(1)}, bf16[1,128,1024]{2,1,0:T(8,128)(2,1)}, u32[]{:S(2)}) copy-start(bf16[1,128,1024]{2,1,0:T(8,128)(2,1)} %param.21) | copy-start | bytes 786436
  112.0 0.7 copy-start.6
  114.2 30.3 %copy-start.19 = (bf16[16,8]{0,1:T(8,128)(2,1)S(1)}, bf16[16,8]{0,1:T(8,128)(2,1)}, u32[]{:S(2)}) copy-start(bf16[16,8]{0,1:T(8,128)(2,1)} %param.32) | copy-start | bytes 772
  114.2 39.5 %all-gather.24.cloned.1.call-start = ((), (), s32[]{:S(2)}) async-start(), calls=%async_computation.13 | async-start | bytes 2359296 | tf_op jit(solution)/shard_map/all_gather | solution.py:219
  114.8 57.5 %all-gather.22.cloned.1.call-start = ((), (), s32[]{:S(2)}) async-start(), calls=%async_computation.12 | async-start | bytes 1310720 | tf_op jit(solution)/shard_map/all_gather | solution.py:252
  143.8 57.5 %all-gather.26.cloned.1.call-start = ((), (), s32[]{:S(2)}) async-start(), calls=%async_computation.14 | async-start | bytes 2359296 | tf_op jit(solution)/shard_map/all_gather | solution.py:220
  144.4 88.6 %reduce-scatter.25.cloned.1.call-start = ((), (), s32[]{:S(2)}) async-start(), calls=%async_computation.15 | async-start | bytes 1310720 | tf_op jit(solution)/shard_map/reduce_scatter | solution.py:256
  201.3 4.3 copy-start.24
  201.3 13.0 %copy-start.25 = (bf16[128]{0:T(256)(128)(2,1)S(1)}, bf16[128]{0:T(256)(128)(2,1)}, u32[]{:S(2)}) copy-start(bf16[128]{0:T(256)(128)(2,1)} %param.35) | copy-start | bytes 772
  201.3 20.9 %copy-start.26 = (bf16[128]{0:T(256)(128)(2,1)S(1)}, bf16[128]{0:T(256)(128)(2,1)}, u32[]{:S(2)}) copy-start(bf16[128]{0:T(256)(128)(2,1)} %param.36) | copy-start | bytes 772
  201.3 31.6 %copy-start.3 = (bf16[128,1024]{1,0:T(8,128)(2,1)S(1)}, bf16[128,1024]{1,0:T(8,128)(2,1)}, u32[]{:S(2)}) copy-start(bf16[128,1024]{1,0:T(8,128)(2,1)} %reduce-scatter.23.cloned.1.call-done) | copy-start | bytes 786436
  205.5 29.0 %copy-start.8 = (bf16[1,128,1024]{2,1,0:T(8,128)(2,1)S(1)}, bf16[1,128,1024]{2,1,0:T(8,128)(2,1)}, u32[]{:S(2)}) copy-start(bf16[1,128,1024]{2,1,0:T(8,128)(2,1)} %param.37) | copy-start | bytes 786436
  205.5 57.0 %all-gather.28.cloned.1.call-start = ((), (), s32[]{:S(2)}) async-start(), calls=%async_computation.16 | async-start | bytes 1310720 | tf_op jit(solution)/shard_map/all_gather | solution.py:269
  235.9 86.2 %all-reduce.15.cloned.1.call-start = ((), (), s32[]{:S(2)}) async-start(), calls=%async_computation.26 | async-start | bytes 2162688
  262.5 4.6 copy-start.27
  267.1 1.3 copy-start.33
  268.5 1.4 copy-start.31
  269.9 82.1 %copy-start.7 = (bf16[512,256]{0,1:T(8,128)(2,1)S(1)}, bf16[512,256]{0,1:T(8,128)(2,1)}, u32[]{:S(2)}) copy-start(bf16[512,256]{0,1:T(8,128)(2,1)} %copy-done.6) | copy-start | bytes 786436
  269.9 82.1 %copy-start.12 = (bf16[256,1024]{1,0:T(8,128)(2,1)S(1)}, bf16[256,1024]{1,0:T(8,128)(2,1)}, u32[]{:S(2)}) copy-start(bf16[256,1024]{1,0:T(8,128)(2,1)} %all_gather.73) | copy-start | bytes 1572868
  269.9 82.1 %all-gather.30.cloned.1.call-start = ((), (), s32[]{:S(2)}) async-start(), calls=%async_computation.17 | async-start | bytes 1310720 | tf_op jit(solution)/shard_map/all_gather | solution.py:297
  324.6 85.0 %reduce-scatter.27.cloned.1.call-start = ((), (), s32[]{:S(2)}) async-start(), calls=%async_computation.18 | async-start | bytes 2621440 | tf_op jit(solution)/shard_map/reduce_scatter | solution.py:169
  379.0 1.2 copy-start.29
  379.0 1.5 copy-start.32
  379.0 75.1 %reduce-scatter.39.cloned.1.call-start = ((), (), s32[]{:S(2)}) async-start(), calls=%async_computation.25 | async-start | bytes 2359296
  387.4 1.3 copy-start.28
  387.4 1.6 copy-start.34
  387.4 111.1 %reduce-scatter.29.cloned.1.call-start = ((), (), s32[]{:S(2)}) async-start(), calls=%async_computation.19 | async-start | bytes 2359296 | tf_op jit(solution)/shard_map/reduce_scatter | solution.py:340
  391.7 2.9 copy-start.2
  391.7 143.9 %reduce-scatter.37.cloned.1.call-start = ((), (), s32[]{:S(2)}) async-start(), calls=%async_computation.24 | async-start | bytes 589824
  394.5 178.3 %reduce-scatter.31.cloned.1.call-start = ((), (), s32[]{:S(2)}) async-start(), calls=%async_computation.21 | async-start | bytes 589824
  396.0 16.1 %copy-start.4 = (f32[128,1024]{1,0:T(8,128)S(1)}, f32[128,1024]{1,0:T(8,128)}, u32[]{:S(2)}) copy-start(f32[128,1024]{1,0:T(8,128)} %get-tuple-element.385) | copy-start | bytes 1572868
  396.1 16.2 %copy-start.15 = (bf16[1024,256]{1,0:T(8,128)(2,1)S(1)}, bf16[1024,256]{1,0:T(8,128)(2,1)}, u32[]{:S(2)}) copy-start(bf16[1024,256]{1,0:T(8,128)(2,1)} %copy-done.14) | copy-start | bytes 1572868
  396.1 213.9 %reduce-scatter.35.cloned.1.call-start = ((), (), s32[]{:S(2)}) async-start(), calls=%async_computation.23 | async-start | bytes 589824
  412.1 2.0 copy-start.5
  412.1 235.0 %reduce-scatter.33.cloned.1.call-start = ((), (), s32[]{:S(2)}) async-start(), calls=%async_computation.22 | async-start | bytes 589824
  414.6 2.6 copy-start.10
  415.7 233.2 %all-reduce.17.cloned.1.call-start = ((), (), s32[]{:S(2)}) async-start(), calls=%async_computation.27 | async-start | bytes 2162688
  419.7 1.3 copy-start.30
Sparse Core Ops, SparseCore 0:
  10.4 30.6 all-gather.31
  43.8 16.0 all-gather.19
  62.0 18.0 all-gather.17
  114.3 25.3 reduce-scatter.22
  205.7 27.2 reduce-scatter.24
  236.0 26.4 all-gather.27
  379.1 30.4 reduce-scatter.26
  413.0 41.0 reduce-scatter.38
  457.4 41.0 reduce-scatter.28
  501.4 34.1 reduce-scatter.36
  538.7 34.1 reduce-scatter.30
  575.8 34.1 reduce-scatter.34
  613.0 34.1 reduce-scatter.32
Sparse Core Ops, SparseCore 1:
  116.6 25.7 all-gather.23
  144.3 27.9 all-gather.21
  174.0 27.3 all-gather.25
  269.9 52.1 all-reduce.14
  324.7 27.2 all-gather.29
  421.1 52.6 all-reduce.16
where the time goes:
time: 688 us; the launch traced here: 687 us
  waiting for transfers between devices  391 us (57%)
  blocking collectives  143 us (21%)
  matrix products  68.1 us (10%)
  local copies, waits for them, and re-layouts  41.3 us (6%)
  other arithmetic  23.8 us (3%)
  between operations  18 us (3%)
    unnamed x26, waiting for transfers between devices  225 us
    reduce_scatter x1, waiting for transfers between devices, local(): lax.psum_scatter(g_inner_w.astype(jnp.bfloat16), ('dp', 'blk'), scatter_d...  42.5 us
    all_gather x1, waiting for transfers between devices, local(): d_one_all = lax.all_gather(d_one_round, 'ulysses', axis=0, tiled=True)  27.2 us
    all_gather x1, waiting for transfers between devices, local(): d_two_all = lax.all_gather(d_two_round, 'ulysses', axis=0, tiled=True)  26.5 us
    unnamed x88, local copies, waits for them, and re-layouts  25.2 us
    all_gather x1, waiting for transfers between devices, local(): lax.all_gather(outer_weight, ('dp', 'blk'), axis=1, tiled=True)  24.1 us
    unnamed x1, blocking collectives  22.5 us
    all_gather x1, waiting for transfers between devices, local(): normed_all = lax.all_gather(normed_round, 'ulysses', axis=0, tiled=True)  18.6 us
  transfers between devices with their start and end apart: 19, of which 15 were waited for; matrix products, arithmetic and copies ran while one was open for 8% of the time, Pallas kernels for 0%

commit v1 on v0

v1 whole, which is shorter than its diff:
```python
import math

import jax
import jax.numpy as jnp
from jax import lax
from jax.experimental import pallas as pl
from jax.experimental.pallas import tpu as pltpu
from jax.sharding import PartitionSpec as P

DH = 64


EPSILON = 1e-05


def gelu_parts(pre):
    cdf = 0.5 * (1.0 + lax.erf(pre * 0.7071067811865476))
    dens = jnp.exp(-0.5 * pre * pre) * 0.3989422804014327
    return (pre * cdf, cdf + pre * dens)


def norm_forward(resid, gain, shift):
    centre = resid - jnp.mean(resid, axis=-1, keepdims=True)
    rstd = lax.rsqrt(jnp.mean(centre * centre, axis=-1, keepdims=True) + EPSILON)
    unit = centre * rstd
    return (unit * gain + shift, unit, rstd)


def norm_backward(grad, unit, rstd, gain):
    scaled = grad * gain
    inner = (
        scaled
        - jnp.mean(scaled, axis=-1, keepdims=True)
        - unit * jnp.mean(scaled * unit, axis=-1, keepdims=True)
    )
    return (rstd * inner, jnp.sum(grad * unit, axis=0), jnp.sum(grad, axis=0))


def mat(left, right):
    return jnp.dot(left, right, preferred_element_type=jnp.float32)


MESH = pl.DeviceIdType.MESH
ORDER = ("dp", "blk", "ulysses")


def here():
    return {name: lax.axis_index(name) for name in ORDER}


def bits_of(axes):
    bits = []
    below = 1
    for name in reversed(axes):
        size = lax.axis_size(name)
        stride = 1
        while stride < size:
            bits.append((name, stride, stride * below))
            stride *= 2
        below *= size
    return bits


def slot_of(axes, at):
    index = 0
    for name in axes:
        index = index * lax.axis_size(name) + at[name]
    return index


def flip(index, stride):
    return index + stride * (1 - 2 * ((index // stride) % 2))


def flip_all(index, bits):
    for bit in bits:
        index = flip(index, bit[2])
    return index


def peer(at, bit):
    name, stride, unused = bit
    return tuple(flip(at[axis], stride) if axis == name else at[axis] for axis in ORDER)


def subsets(bits):
    found = [()]
    for bit in bits:
        found = found + [sub + (bit,) for sub in found]
    return found


def row_parts(rows, size, tile):
    if size < 65536 or rows % (2 * tile):
        return [(0, rows)]
    return [(0, rows // 2), (rows // 2, rows // 2)]


def row_loop(rows, body):
    step = math.gcd(rows, 64)

    def turn(i, carry):
        body(pl.ds(pl.multiple_of(i * step, step), step))
        return carry

    lax.fori_loop(0, rows // step, turn, 0)


class Sems:
    def __init__(self, ref=None):
        self.ref, self.count = ref, 0

    def take(self):
        self.count += 1
        return self.count - 1 if self.ref is None else self.ref.at[self.count - 1]


def remote(src, dst, sems, to):
    return pltpu.make_async_remote_copy(
        src_ref=src, dst_ref=dst, send_sem=sems[0], recv_sem=sems[1], device_id=to, device_id_type=MESH
    )


class CubeGather:
    def __init__(self, axes, arrays):
        self.axes, self.arrays, self.bits = axes, list(arrays), bits_of(axes)
        self.slots = math.prod(lax.axis_size(name) for name in axes)
        self.outs = [jax.ShapeDtypeStruct((self.slots,) + a.shape, a.dtype) for a in self.arrays]
        self.scratch = []
        streams = sum(len(self.parts(a)) for a in self.arrays)
        self.sems = 2 * streams * (self.slots - 1)

    def parts(self, array):
        return row_parts(array.shape[0], array.size, 16)

    def peers(self, at):
        return [(peer(at, bit), None) for bit in self.bits]

    def run(self, at, ins, outs, scratch, sems):
        gens = []
        me = slot_of(self.axes, at)
        for array, src, dst in zip(self.arrays, ins, outs):
            for number, part in enumerate(self.parts(array)):
                far = self.bits[1:]
                order = (far if number else far[::-1]) + self.bits[:1]
                gens.append(self.stream(at, me, src, dst, part, order, sems))
        yield from together(gens)
        for src, dst in zip(ins, outs):
            dst[me] = src[...]

    def stream(self, at, me, src, dst, part, order, sems):
        rows = pl.ds(*part)
        held, landing, sent = [()], {}, []
        for bit in order:
            fresh = {}
            for sub in held:
                if sub in landing:
                    landing.pop(sub).wait_recv()
                slot = flip_all(me, sub)
                there = dst.at[slot, rows]
                copy = remote(
                    there if sub else src.at[rows], there, (sems.take(), sems.take()), peer(at, bit)
                )
                copy.start()
                sent.append(copy)
                fresh[sub + (bit,)] = copy
            landing.update(fresh)
            held = held + list(fresh)
            yield
        for copy in landing.values():
            copy.wait_recv()
        for copy in sent:
            copy.wait_send()


class CubeScatter:
    def __init__(self, axes, arrays):
        self.axes, self.arrays, self.bits = axes, list(arrays), bits_of(axes)
        self.slots = math.prod(lax.axis_size(name) for name in axes)
        self.outs = [jax.ShapeDtypeStruct(a.shape[1:], jnp.float32) for a in self.arrays]
        self.scratch = []
        self.sems = 0
        for a in self.arrays:
            for part in self.parts(a):
                left = self.slots
                for unused in self.bits:
                    left //= 2
                    self.scratch.append(((left, part[1], a.shape[2]), a.dtype))
                    if left > 1:
                        self.scratch.append(((left, part[1], a.shape[2]), a.dtype))
                self.sems += 2 * (self.slots - 1)

    def parts(self, array):
        return row_parts(array.shape[1], array.size // self.slots, 16)

    def peers(self, at):
        return [(peer(at, bit), None) for bit in self.bits]

    def run(self, at, ins, outs, scratch, sems):
        gens = []
        me = slot_of(self.axes, at)
        scratch = list(scratch)
        for array, src, dst in zip(self.arrays, ins, outs):
            for number, part in enumerate(self.parts(array)):
                far = self.bits[1:]
                order = self.bits[:1] + (far if number else far[::-1])
                own = scratch[: 2 * len(order) - 1]
                scratch = scratch[2 * len(order) - 1 :]
                gens.append(self.stream(at, me, src, dst, part, order, own, sems))
        yield from together(gens)

    def stream(self, at, me, src, dst, part, order, scratch, sems):
        start, count = part
        rows = pl.ds(start, count)
        level = None
        sent = []
        for stage, bit in enumerate(order):
            rest = order[stage + 1 :]
            subs = subsets(rest)
            before = subsets(order[stage:])
            landed = scratch[2 * stage]
            copies = []
            for j, sub in enumerate(subs):
                if level is None:
                    piece = src.at[flip_all(flip(me, bit[2]), sub), rows]
                else:
                    piece = level.at[before.index((bit,) + sub)]
                copy = remote(piece, landed.at[j], (sems.take(), sems.take()), peer(at, bit))
                copy.start()
                copies.append(copy)
            sent += copies
            yield
            goal = None if not rest else scratch[2 * stage + 1]
            for j, sub in enumerate(subs):
                copies[j].wait_recv()
                slot = None if level is not None else flip_all(me, sub)
                old = None if level is None else before.index(sub)

                def add(here_rows, j=j, slot=slot, old=old, level=level, goal=goal, landed=landed):
                    moved = pl.ds(start + here_rows.start, here_rows.size)
                    mine = src[slot, moved, :] if level is None else level[old, here_rows, :]
                    total = mine.astype(jnp.float32) + landed[j, here_rows, :].astype(jnp.float32)
                    if goal is None:
                        dst[moved, :] = total
                    else:
                        goal[j, here_rows, :] = total.astype(goal.dtype)

                row_loop(count, add)
            level = goal
        for copy in sent:
            copy.wait_send()


def line_peers(at, size):
    spot = at["ulysses"]
    return [
        ((at["dp"], at["blk"], spot + 1), spot < size - 1),
        ((at["dp"], at["blk"], spot - 1), spot > 0),
    ]


class LineGather:
    def __init__(self, arrays):
        self.arrays, self.size = list(arrays), lax.axis_size("ulysses")
        self.outs = [jax.ShapeDtypeStruct((self.size,) + a.shape, a.dtype) for a in self.arrays]
        self.scratch = []
        streams = sum(len(self.parts(a)) for a in self.arrays)
        self.sems = streams * 4 * (self.size - 1)

    def parts(self, array):
        return row_parts(array.shape[0], array.size, 16)

    def peers(self, at):
        return line_peers(at, self.size)

    def run(self, at, ins, outs, scratch, sems):
        gens = [
            self.stream(at, src, dst, part, sems)
            for array, src, dst in zip(self.arrays, ins, outs)
            for part in self.parts(array)
        ]
        yield from together(gens)
        for src, dst in zip(ins, outs):
            dst[at["ulysses"]] = src[...]

    def stream(self, at, src, dst, part, sems):
        size, spot = self.size, at["ulysses"]
        rows = pl.ds(*part)
        ways = []
        for sign in (1, -1):
            tail = spot if sign > 0 else size - 1 - spot
            to = (at["dp"], at["blk"], spot + sign)
            pairs = [(sems.take(), sems.take()) for unused in range(size - 1)]
            ways.append((sign, tail, to, pairs))

        def copy(way, step):
            sign, tail, to, pairs = way
            slot = spot - sign * step
            there = dst.at[slot, rows]
            return remote(src.at[rows] if step == 0 else there, there, pairs[step], to)

        for step in range(size):
            for way in ways:
                tail = way[1]
                if step > 0:

                    @pl.when(tail >= step)
                    def unused_wait(way=way, step=step):
                        copy(way, step - 1).wait_recv()

                if step < size - 1:

                    @pl.when(jnp.logical_and(tail < size - 1, tail >= step))
                    def unused_send(way=way, step=step):
                        copy(way, step).start()

            yield
        for way in ways:
            for step in range(size - 1):

                @pl.when(jnp.logical_and(way[1] < size - 1, way[1] >= step))
                def unused_sent(way=way, step=step):
                    copy(way, step).wait_send()


class LineScatter:
    def __init__(self, arrays):
        self.arrays, self.size = list(arrays), lax.axis_size("ulysses")
        self.outs = [jax.ShapeDtypeStruct(a.shape[1:], jnp.float32) for a in self.arrays]
        self.scratch = []
        self.sems = 0
        for a in self.arrays:
            for part in self.parts(a):
                shape = (2, 2, self.size - 1, part[1], a.shape[2])
                self.scratch.append((shape, a.dtype))
                self.sems += 4 * (self.size - 1)

    def parts(self, array):
        return row_parts(array.shape[1], array.size // self.size, 16)

    def peers(self, at):
        return line_peers(at, self.size)

    def run(self, at, ins, outs, scratch, sems):
        gens, scratch = [], list(scratch)
        for array, src, dst in zip(self.arrays, ins, outs):
            for part in self.parts(array):
                gens.append(self.stream(at, src, dst, part, scratch.pop(0), sems))
        yield from together(gens)

    def stream(self, at, src, dst, part, room, sems):
        size, spot = self.size, at["ulysses"]
        start, count = part
        ways = []
        for index, sign in enumerate((1, -1)):
            tail = spot if sign > 0 else size - 1 - spot
            to = (at["dp"], at["blk"], spot + sign)
            pairs = [(sems.take(), sems.take()) for unused in range(size - 1)]
            ways.append((index, sign, tail, to, pairs))

        def owner(way, step):
            return spot + way[1] * (size - 1 - step)

        def copy(way, step, first):
            index, sign, tail, to, pairs = way
            piece = src.at[owner(way, step), pl.ds(start, count)] if first else room.at[index, 1, step]
            return remote(piece, room.at[index, 0, step], pairs[step], to)

        for step in range(size - 1):
            for way in ways:

                @pl.when(way[2] == 0)
                def unused_first(way=way, step=step):
                    copy(way, step, True).start()

                if step > 0:

                    @pl.when(jnp.logical_and(way[2] >= 1, way[2] <= step))
                    def unused_next(way=way, step=step):
                        index = way[0]
                        copy(way, step - 1, False).wait_recv()

                        def add(rows):
                            moved = pl.ds(start + rows.start, rows.size)
                            total = src[owner(way, step), moved, :].astype(jnp.float32) + room[
                                index, 0, step - 1, rows, :
                            ].astype(jnp.float32)
                            room[index, 1, step, rows, :] = total.astype(room.dtype)

                        row_loop(count, add)
                        copy(way, step, False).start()

            yield

        def begin(rows):
            moved = pl.ds(start + rows.start, rows.size)
            dst[moved, :] = src[spot, moved, :].astype(jnp.float32)

        row_loop(count, begin)
        for way in ways:

            @pl.when(way[2] >= 1)
            def unused_last(way=way):
                copy(way, size - 2, False).wait_recv()

                def add(rows):
                    moved = pl.ds(start + rows.start, rows.size)
                    dst[moved, :] = dst[moved, :] + room[way[0], 0, size - 2, rows, :].astype(jnp.float32)

                row_loop(count, add)

        for way in ways:
            for step in range(size - 1):

                @pl.when(way[2] == 0)
                def unused_sent_first(way=way, step=step):
                    copy(way, step, True).wait_send()

                if step > 0:

                    @pl.when(jnp.logical_and(way[2] >= 1, way[2] <= step))
                    def unused_sent(way=way, step=step):
                        copy(way, step, False).wait_send()


def together(gens):
    gens = list(gens)
    while gens:
        alive = []
        for gen in gens:
            try:
                next(gen)
                alive.append(gen)
            except StopIteration:
                pass
        gens = alive
        if gens:
            yield


def communicate(number, tasks):
    arrays = [a for task in tasks for a in task.arrays]
    outs = [o for task in tasks for o in task.outs]
    rooms = [s for task in tasks for s in task.scratch]
    count = sum(task.sems for task in tasks)

    def kernel(*refs):
        ins, refs = refs[: len(arrays)], refs[len(arrays) :]
        results, refs = refs[: len(outs)], refs[len(outs) :]
        scratch, sem_ref = refs[: len(rooms)], refs[len(rooms)]
        at = here()
        barrier = pltpu.get_barrier_semaphore()
        total = 0
        seen = set()
        for task in tasks:
            kind = type(task) in (LineGather, LineScatter)
            for place, (to, exists) in enumerate(task.peers(at)):
                name = ("line", place) if kind else task.bits[place][:2]
                if name in seen:
                    continue
                seen.add(name)
                if exists is None:
                    pl.semaphore_signal(barrier, inc=1, device_id=to, device_id_type=MESH)
                    total = total + 1
                else:

                    @pl.when(exists)
                    def unused_greet(to=to):
                        pl.semaphore_signal(barrier, inc=1, device_id=to, device_id_type=MESH)

                    total = total + exists.astype(jnp.int32)
        pl.semaphore_wait(barrier, total)
        sems = Sems(sem_ref)
        gens = []
        for task in tasks:
            n_in, n_out, n_room = len(task.arrays), len(task.outs), len(task.scratch)
            gens.append(task.run(at, ins[:n_in], results[:n_out], scratch[:n_room], sems))
            ins, results, scratch = ins[n_in:], results[n_out:], scratch[n_room:]
        for unused in together(gens):
            pass

    flat = pl.pallas_call(
        kernel,
        name="exchange_%d" % number,
        out_shape=outs,
        in_specs=[pl.BlockSpec(memory_space=pltpu.VMEM)] * len(arrays),
        out_specs=[pl.BlockSpec(memory_space=pltpu.VMEM)] * len(outs),
        scratch_shapes=[pltpu.VMEM(*room) for room in rooms] + [pltpu.SemaphoreType.DMA((count,))],
        compiler_params=pltpu.CompilerParams(collective_id=number, has_side_effects=True),
    )(*arrays)
    flat = list(flat)
    split = []
    for task in tasks:
        split.append(flat[: len(task.outs)])
        flat = flat[len(task.outs) :]
    return split


def pack(pieces, slots):
    joined = jnp.concatenate([p.astype(jnp.float32) for p in pieces], axis=1)
    length = joined.shape[1]
    padded = -(-length // 1024) * 1024
    return jnp.pad(joined, ((0, 0), (0, padded - length))).reshape(slots, padded // 128, 128)


def row_slots(grad, slots):
    return grad.astype(jnp.bfloat16).reshape(slots, -1, grad.shape[1])


def column_slots(grad, slots):
    return grad.astype(jnp.bfloat16).reshape(grad.shape[0], slots, -1).transpose(1, 0, 2)


def spread_rows(vectors, lanes):
    rows = jnp.pad(jnp.stack(vectors), ((0, -len(vectors) % 8), (0, 0)))
    return jnp.broadcast_to(rows[None], (lanes,) + rows.shape)


def attend_forward(q_heads, k_all, v_all, heads_dev):
    rows, head_width = q_heads.shape
    scale = DH ** (-0.5)
    q_three = q_heads.reshape(rows, heads_dev, DH)

    def fold(carry, piece, start):
        k_piece, v_piece = piece
        count = k_piece.shape[0]
        size = math.gcd(count, 512)
        steps = count // size
        k_split = k_piece.reshape(steps, size, heads_dev, DH)
        v_split = v_piece.reshape(steps, size, heads_dev, DH)

        def step(state, blocks):
            best, total, accum = state
            k_block, v_block = blocks
            scores = (
                jnp.einsum("qhd,khd->hqk", q_three, k_block, preferred_element_type=jnp.float32)
                * scale
            )
            new_best = jnp.maximum(best, jnp.max(scores, axis=-1))
            fade = jnp.exp(best - new_best)
            weights = jnp.exp(scores - new_best[:, :, None])
            total = total * fade + jnp.sum(weights, axis=-1)
            update = jnp.einsum("hqk,khd->qhd", weights, v_block.astype(jnp.float32))
            accum = accum.reshape(rows, heads_dev, DH) * fade.T[:, :, None] + update
            return ((new_best, total, accum.reshape(rows, head_width)), None)

        state, unused = lax.scan(step, carry, (k_split, v_split))
        return state

    start_state = (
        jnp.full((heads_dev, rows), -jnp.inf, jnp.float32),
        jnp.zeros((heads_dev, rows), jnp.float32),
        jnp.zeros((rows, head_width), jnp.float32),
    )
    best, total, accum = fold(
        start_state,
        (
            k_all,
            v_all,
        ),
        jnp.int32(0),
    )
    attended = (accum.reshape(rows, heads_dev, DH) / total.T[:, :, None]).reshape(rows, head_width)
    return (attended.astype(jnp.bfloat16), best + jnp.log(total))


def attend_backward(q_heads, k_all, v_all, attended, lse, d_att, heads_dev):
    rows, head_width = q_heads.shape
    scale = DH ** (-0.5)
    q_three = q_heads.reshape(rows, heads_dev, DH)
    do_three = d_att.reshape(rows, heads_dev, DH)
    delta = (
        (d_att.astype(jnp.float32) * attended.astype(jnp.float32))
        .reshape(rows, heads_dev, DH)
        .sum(-1)
        .T
    )
    all_keys = rows * lax.axis_size("blk")

    def fold(carry, piece, start):
        dq_accum, key_accum = carry
        k_piece, v_piece = piece
        count = k_piece.shape[0]
        size = math.gcd(count, 512)
        steps = count // size
        k_split = k_piece.reshape(steps, size, heads_dev, DH)
        v_split = v_piece.reshape(steps, size, heads_dev, DH)

        def step(dq_state, blocks):
            k_block, v_block = blocks
            scores = (
                jnp.einsum("qhd,khd->hqk", q_three, k_block, preferred_element_type=jnp.float32)
                * scale
            )
            weights = jnp.exp(scores - lse[:, :, None])
            weights_round = weights.astype(jnp.bfloat16)
            v_part = jnp.einsum(
                "hqk,qhd->khd", weights_round, do_three, preferred_element_type=jnp.float32
            )
            d_weights = jnp.einsum(
                "qhd,khd->hqk", do_three, v_block, preferred_element_type=jnp.float32
            )
            d_scores = (weights * (d_weights - delta[:, :, None])).astype(jnp.bfloat16)
            q_part = (
                jnp.einsum("hqk,khd->qhd", d_scores, k_block, preferred_element_type=jnp.float32)
                * scale
            )
            k_part = (
                jnp.einsum("hqk,qhd->khd", d_scores, q_three, preferred_element_type=jnp.float32)
                * scale
            )
            dq_state = dq_state + q_part.reshape(rows, head_width)
            both = (
                k_part.reshape(size, head_width).astype(jnp.bfloat16),
                v_part.reshape(size, head_width).astype(jnp.bfloat16),
            )
            return (dq_state, both)

        dq_accum, parts = lax.scan(step, dq_accum, (k_split, v_split))
        return (dq_accum, parts)

    start_state = (
        jnp.zeros((rows, head_width), jnp.float32),
        None,
    )
    dq_accum, key_accum = fold(
        start_state,
        (
            k_all,
            v_all,
        ),
        jnp.int32(0),
    )
    blocks = lax.axis_size("blk")
    owned = communicate(
        8, [CubeScatter(("blk",), [part.reshape(blocks, rows, head_width) for part in key_accum])]
    )[0]
    return (
        dq_accum.astype(jnp.bfloat16),
        owned[0].astype(jnp.bfloat16),
        owned[1].astype(jnp.bfloat16),
    )


def local(
    tokens,
    query_weight,
    key_weight,
    value_weight,
    out_weight,
    query_bias,
    value_bias,
    out_bias,
    norm1_gain,
    norm1_shift,
    inner_weight,
    inner_bias,
    outer_weight,
    outer_bias,
    norm2_gain,
    norm2_shift,
    out_grad,
):
    group = ("dp", "blk")
    slots = lax.axis_size("dp") * lax.axis_size("blk")
    blocks = lax.axis_size("blk")
    lanes = lax.axis_size("ulysses")
    rows_in = tokens[0]
    tok_rows, width = rows_in.shape
    head_width = query_weight.shape[1]
    heads_dev = head_width // DH
    inner_width = inner_weight.shape[1]
    small_in = (
        out_bias,
        norm1_gain,
        norm1_shift,
        outer_bias,
        norm2_gain,
        norm2_shift,
        query_bias,
        value_bias,
        inner_bias,
    )
    (tok_all,), (q3, k3, v3, o3, small) = communicate(
        0,
        [
            LineGather([rows_in]),
            CubeGather(
                group,
                [
                    query_weight,
                    key_weight,
                    value_weight,
                    out_weight,
                    pack([a.reshape(1, -1) for a in small_in], 1)[0],
                ],
            ),
        ],
    )
    rows_all = tok_all.reshape(-1, width)
    w_query, w_key, w_value = (w.reshape(width, head_width) for w in (q3, k3, v3))
    w_out = o3.transpose(1, 0, 2).reshape(head_width, width)
    flat = small.reshape(slots, -1)
    vectors = []
    start = 0
    for a in small_in:
        piece = flat[:, start : start + a.size]
        start += a.size
        if a.ndim == 2:
            piece = piece.reshape((slots,) + a.shape).transpose(1, 0, 2)
        vectors.append(piece.reshape(-1))
    b_out, gain_one, shift_one, b_outer, gain_two, shift_two, b_query, b_value, b_inner = vectors
    q_heads = (mat(rows_all, w_query) + b_query).astype(jnp.bfloat16)
    k_heads = mat(rows_all, w_key).astype(jnp.bfloat16)
    v_heads = (mat(rows_all, w_value) + b_value).astype(jnp.bfloat16)
    k_all, v_all = communicate(1, [CubeGather(("blk",), [k_heads, v_heads])])[0]
    k_all = k_all.reshape(-1, head_width)
    v_all = v_all.reshape(-1, head_width)
    attended, lse = attend_forward(q_heads, k_all, v_all, heads_dev)
    (attn_sum,), (inner3, outer3) = communicate(
        2,
        [
            LineScatter([mat(attended, w_out).astype(jnp.bfloat16).reshape(lanes, tok_rows, width)]),
            CubeGather(group, [inner_weight, outer_weight]),
        ],
    )
    w_inner = inner3.reshape(width, inner_width)
    w_outer = outer3.transpose(1, 0, 2).reshape(inner_width, width)
    resid_one = rows_in.astype(jnp.float32) + attn_sum + b_out
    normed_one, unit_one, rstd_one = norm_forward(
        resid_one, gain_one, shift_one
    )
    normed_round = normed_one.astype(jnp.bfloat16)
    normed_all = communicate(3, [LineGather([normed_round])])[0][0].reshape(-1, width)
    pre_act = mat(normed_all, w_inner) + b_inner
    act_full, slope = gelu_parts(pre_act)
    activation = act_full.astype(jnp.bfloat16)
    ffn_term = mat(activation, w_outer).astype(jnp.bfloat16).reshape(lanes, tok_rows, width)
    ffn_sum = communicate(4, [LineScatter([ffn_term])])[0][0]
    resid_two = normed_one + ffn_sum + b_outer
    final, unit_two, rstd_two = norm_forward(
        resid_two, gain_two, shift_two
    )
    block_out = final.astype(jnp.bfloat16)[None]
    d_resid_two, g_gain_two, g_shift_two = norm_backward(
        out_grad[0].astype(jnp.float32), unit_two, rstd_two, gain_two
    )
    g_outer_b = jnp.sum(d_resid_two, axis=0)
    d_two_round = d_resid_two.astype(jnp.bfloat16)
    d_two_all = communicate(5, [LineGather([d_two_round])])[0][0].reshape(-1, width)
    g_outer_w = jnp.einsum("tf,td->fd", activation, d_two_all, preferred_element_type=jnp.float32)
    d_pre = jnp.einsum("td,fd->tf", d_two_all, w_outer, preferred_element_type=jnp.float32) * slope
    d_pre_round = d_pre.astype(jnp.bfloat16)
    g_inner_w = jnp.einsum("td,tf->df", normed_all, d_pre_round, preferred_element_type=jnp.float32)
    g_inner_b = jnp.sum(d_pre, axis=0).reshape(-1, DH)
    extras_two = spread_rows([g_gain_two, g_shift_two, g_outer_b], lanes)
    d_term = jnp.einsum("tf,df->td", d_pre_round, w_inner, preferred_element_type=jnp.float32)
    (d_sum, sums_two), (r_outer,) = communicate(
        6,
        [
            LineScatter([d_term.astype(jnp.bfloat16).reshape(lanes, tok_rows, width), extras_two]),
            CubeScatter(group, [column_slots(g_outer_w, slots)]),
        ],
    )
    d_normed = d_resid_two + d_sum
    d_resid_one, g_gain_one, g_shift_one = norm_backward(
        d_normed, unit_one, rstd_one, gain_one
    )
    g_out_b = jnp.sum(d_resid_one, axis=0)
    d_one_round = d_resid_one.astype(jnp.bfloat16)
    (d_one_all,), (r_inner,) = communicate(
        7,
        [LineGather([d_one_round]), CubeScatter(group, [row_slots(g_inner_w, slots)])],
    )
    d_one_all = d_one_all.reshape(-1, width)
    g_out_w = jnp.einsum("te,td->ed", attended, d_one_all, preferred_element_type=jnp.float32)
    d_att = jnp.einsum("td,ed->te", d_one_all, w_out, preferred_element_type=jnp.float32).astype(
        jnp.bfloat16
    )
    dq_heads, dk_heads, dv_heads = attend_backward(
        q_heads, k_all, v_all, attended, lse, d_att, heads_dev
    )
    g_query_w = jnp.einsum("td,te->de", rows_all, dq_heads, preferred_element_type=jnp.float32)
    g_key_w = jnp.einsum("td,te->de", rows_all, dk_heads, preferred_element_type=jnp.float32)
    g_value_w = jnp.einsum("td,te->de", rows_all, dv_heads, preferred_element_type=jnp.float32)
    g_query_b = jnp.sum(dq_heads.astype(jnp.float32), axis=0).reshape(-1, DH)
    g_value_b = jnp.sum(dv_heads.astype(jnp.float32), axis=0).reshape(-1, DH)
    extras_one = spread_rows([g_gain_one, g_shift_one, g_out_b], lanes)
    back = None
    for grad, weight in ((dq_heads, w_query), (dk_heads, w_key), (dv_heads, w_value)):
        term = jnp.einsum("te,de->td", grad, weight, preferred_element_type=jnp.float32)
        back = term if back is None else back + term
    (back_sum, sums_one), (r_query, r_key, r_value, r_out) = communicate(
        9,
        [
            LineScatter([back.astype(jnp.bfloat16).reshape(lanes, tok_rows, width), extras_one]),
            CubeScatter(
                group,
                [
                    row_slots(g_query_w, slots),
                    row_slots(g_key_w, slots),
                    row_slots(g_value_w, slots),
                    column_slots(g_out_w, slots),
                ],
            ),
        ],
    )
    tokens_grad = (d_resid_one + back_sum).astype(jnp.bfloat16)[None]
    small_out = [v.reshape(slots, -1) for v in (*sums_one[:3], *sums_two[:3])]
    for bias in (g_query_b, g_value_b, g_inner_b):
        count = bias.shape[0]
        small_out.append(bias.reshape(count, slots, -1).transpose(1, 0, 2).reshape(slots, -1))
    kept = communicate(10, [CubeScatter(group, [pack(small_out, slots)])])[0][0].reshape(-1)
    ends = []
    start = 0
    for piece in small_out:
        ends.append(kept[start : start + piece.shape[1]])
        start += piece.shape[1]
    gain1, shift1, outb, gain2, shift2, outerb, queryb, valueb, innerb = ends
    return (
        block_out,
        tokens_grad,
        r_query,
        r_key,
        r_value,
        r_out,
        queryb.reshape(query_bias.shape),
        valueb.reshape(value_bias.shape),
        outb,
        gain1,
        shift1,
        r_inner,
        innerb.reshape(inner_bias.shape),
        r_outer,
        outerb,
        gain2,
        shift2,
    )


def solution(mesh):
    in_specs = (
        P("dp", ("blk", "ulysses"), None),
        P(("dp", "blk"), "ulysses"),
        P(("dp", "blk"), "ulysses"),
        P(("dp", "blk"), "ulysses"),
        P("ulysses", ("dp", "blk")),
        P("ulysses", ("dp", "blk")),
        P("ulysses", ("dp", "blk")),
        P(("dp", "blk")),
        P(("dp", "blk")),
        P(("dp", "blk")),
        P(("dp", "blk"), "ulysses"),
        P("ulysses", ("dp", "blk")),
        P("ulysses", ("dp", "blk")),
        P(("dp", "blk")),
        P(("dp", "blk")),
        P(("dp", "blk")),
        P("dp", ("blk", "ulysses"), None),
    )
    out_specs = (
        P("dp", ("blk", "ulysses"), None),
        P("dp", ("blk", "ulysses"), None),
        P(("dp", "blk"), "ulysses"),
        P(("dp", "blk"), "ulysses"),
        P(("dp", "blk"), "ulysses"),
        P("ulysses", ("dp", "blk")),
        P("ulysses", ("dp", "blk")),
        P("ulysses", ("dp", "blk")),
        P(("dp", "blk")),
        P(("dp", "blk")),
        P(("dp", "blk")),
        P(("dp", "blk"), "ulysses"),
        P("ulysses", ("dp", "blk")),
        P("ulysses", ("dp", "blk")),
        P(("dp", "blk")),
        P(("dp", "blk")),
        P(("dp", "blk")),
    )
    return jax.shard_map(local, mesh=mesh, in_specs=in_specs, out_specs=out_specs, check_vma=False)
```

time: 688 us -> 403 us (0.59)
  waiting for transfers between devices: 391 us -> 0 us
  Pallas kernels: 0 us -> 236 us
  blocking collectives: 143 us -> 0 us
  matrix products: 68.1 us -> 105 us
  between operations: 18 us -> 1.26 us
  other arithmetic: 23.8 us -> 13.4 us
    pallas_call x0 -> x11, Pallas kernels: none -> 236 us  [communicate(): pl.pallas_call(kernel, name='exchange_%d' % number, out_shape=outs, in_sp...]
    unnamed x26 -> x0, waiting for transfers between devices: 225 us -> none
    all_gather x13 -> x0, blocking collectives: 121 us -> none  [the longest x1 11.2 us: local(): lax.all_gather(out_weight, ('dp', 'blk'), axis=1, tiled=True)]
    all_gather x8 -> x0, waiting for transfers between devices: 108 us -> none  [the longest x1 27.2 us: local(): d_one_all = lax.all_gather(d_one_round, 'ulysses', axis=0, tiled=True)]
    reduce_scatter x4 -> x0, waiting for transfers between devices: 58.3 us -> none  [the longest x1 42.5 us: local(): lax.psum_scatter(g_inner_w.astype(jnp.bfloat16), ('dp', 'blk'), scatter_d...]
    unnamed x1 -> x0, blocking collectives: 22.5 us -> none
    unnamed x88 -> x65, local copies, waits for them, and re-layouts: 25.2 us -> 8.57 us
    dot_general x8, matrix products: 6.13 us -> 21.4 us  [step(): jnp.einsum('qhd,khd->hqk', q_three, k_block, preferred_element_type=jnp.f...]
  transfers between devices with their start and end apart: 19 -> 0, of which waited for: 15 -> 0; matrix products, arithmetic and copies ran while one was open for 8% -> 0% of each run, Pallas kernels for 0% -> 0%
where the time goes in v1:
time: 403 us; the launch traced here: 399 us
  Pallas kernels  236 us (59%)
  matrix products  105 us (26%)
  local copies, waits for them, and re-layouts  43 us (11%)
  other arithmetic  13.4 us (3%)
    pallas_call x11, Pallas kernels, communicate(): pl.pallas_call(kernel, name='exchange_%d' % number, out_shape=outs, in_sp...  236 us
    dot_general x8, matrix products, step(): jnp.einsum('qhd,khd->hqk', q_three, k_block, preferred_element_type=jnp.f...  21.4 us
    dot_general x6, matrix products, mat(): return jnp.dot(left, right, preferred_element_type=jnp.float32)  14.7 us
    dot_general x4, matrix products, step(): update = jnp.einsum('hqk,khd->qhd', weights, v_block.astype(jnp.float32))  13.4 us
    dot_general x4, matrix products, step(): jnp.einsum('hqk,qhd->khd', weights_round, do_three, preferred_element_typ...  12.2 us
    dynamic_update_slice x12, local copies, waits for them, and re-layouts, fold(): dq_accum, parts = lax.scan(step, dq_accum, (k_split, v_split))  11.1 us
    dot_general x4, matrix products, step(): jnp.einsum('qhd,khd->hqk', do_three, v_block, preferred_element_type=jnp....  10.6 us
    unnamed x65, local copies, waits for them, and re-layouts  8.57 us

profile of v1, /device:TPU:0, one launch (start us, length us, event | category | flops | bytes accessed | tf_op | source)
XLA Modules:
  0.0 399.1 jit_solution(7053238452762094001)
XLA Ops:
  4.5 27.9 %exchange_0.1 = (bf16[4,128,1024]{2,1,0:T(8,128)(2,1)}, bf16[8,128,256]{2,1,0:T(8,128)(2,1)}, bf16[8,128,256]{2,1,0:T(8,128)(2,1)}, bf16[8,128,256]{2,1,0:T(8,12...) custom-call(bf16[128,1024]{1,0:T(8,128)(2,1)} %bitcast.278, bf16[128,256]{1,0:T(8,128)(2,1)} %refs_1_.2, ...), custom_call_target="tpu_custom_call" | custom-call | tf_op jit(solution)/shard_map/exchange_0/pallas_call | solution.py:482
  33.5 2.5 fusion.47.refs_1_
  36.0 1.1 convolution_convert_fusion.10.refs_0_
  37.2 17.8 %exchange_1.1 = (bf16[4,512,256]{2,1,0:T(8,128)(2,1)}, bf16[4,512,256]{2,1,0:T(8,128)(2,1)}) custom-call(bf16[512,256]{1,0:T(8,128)(2,1)} %convolution_convert_fusion.10.refs_0_, bf16[512,256]{1,0:T(8,128)(2,1)} %fusion.47.refs_1_), custom_call_target="tpu_custom_call" | custom-call | tf_op jit(solution)/shard_map/exchange_1/pallas_call | solution.py:482
  55.0 2.4 copy.62
  57.4 1.3 copy.64
  59.5 31.8 %while.30 = (s32[]{:T(128)}, f32[4,512]{1,0:T(4,128)S(1)}, f32[4,512]{1,0:T(4,128)S(1)}, f32[512,256]{0,1:T(8,128)S(1)}, bf16[4,512,4,64]{1,3,2,0:T(8,128)(2,1)}...) while((s32[]{:T(128)}, f32[4,512]{1,0:T(4,128)S(1)}, ...), condition=%wide.region_3.4_spmd.clone, body=%wide.region_0.3_spmd.clone.sunk | while | flops 276049920 | bytes 31327364 | solution.py:547
  59.5 3.7 bitcast_reduce_fusion.3
  63.2 3.3 fusion.145
  67.5 3.6 bitcast_reduce_fusion.3
  71.1 3.3 fusion.145
  75.4 3.6 bitcast_reduce_fusion.3
  79.1 3.3 fusion.145
  83.3 3.6 bitcast_reduce_fusion.3
  87.0 3.3 fusion.145
  91.5 1.5 convolution_convert_fusion.4
  93.0 26.0 %exchange_2.1 = (f32[128,1024]{1,0:T(8,128)}, bf16[8,128,1024]{2,1,0:T(8,128)(2,1)}, bf16[8,1024,128]{2,1,0:T(8,128)(2,1)}) custom-call(bf16[4,128,1024]{2,1,0:T(8,128)(2,1)} %bitcast.261, bf16[128,1024]{1,0:T(8,128)(2,1)} %refs_1_.3, bf16[1024,128]{1,0:T(8,128)(2,1)} %refs_2_.3), custom_call_target="tpu_custom_call" | custom-call | tf_op jit(solution)/shard_map/exchange_2/pallas_call | solution.py:482
  119.1 1.2 fusion.76
  121.4 23.8 %exchange_3.1 = bf16[4,128,1024]{2,1,0:T(8,128)(2,1)} custom-call(bf16[128,1024]{1,0:T(8,128)(2,1)} %fusion.61.refs_0_), custom_call_target="tpu_custom_call" | custom-call | tf_op jit(solution)/shard_map/exchange_3/pallas_call | solution.py:482
  145.5 4.9 %multiply_convert_fusion.1 = (bf16[512,1024]{1,0:T(8,128)(2,1)}, f32[512,1024]{1,0:T(8,128)}) fusion(f32[1024]{0:T(1024)S(1)} %add.153, bf16[512,1024]{1,0:T(8,128)(2,1)} %bitcast.274, bf16[1024,1024]{1,0:T(8,128)(2,1)} %bitcast.326), kind=kOutput, calls=%fused_computation.53 | convolution fusion | flops 1076887552 | bytes 6295552 | tf_op jit(solution)/shard_map/dot_general | solution.py:40
  150.4 3.9 copy.67
  154.3 4.2 %convolution_convert_fusion.3 = bf16[512,1024]{1,0:T(8,128)(2,1)} fusion(bf16[512,1024]{1,0:T(8,128)(2,1)} %get-tuple-element.352, bf16[1024,1024]{0,1:T(8,128)(2,1)} %bitcast.267), kind=kOutput, calls=%fused_computation.58 | convolution fusion | flops 1074266112 | bytes 4194304 | tf_op jit(solution)/shard_map/dot_general | solution.py:40
  158.5 20.1 %exchange_4.1 = f32[128,1024]{1,0:T(8,128)} custom-call(bf16[4,128,1024]{2,1,0:T(8,128)(2,1)} %bitcast.279), custom_call_target="tpu_custom_call" | custom-call | tf_op jit(solution)/shard_map/exchange_4/pallas_call | solution.py:482
  178.6 1.3 fusion.75
  182.2 20.4 %exchange_5.1 = bf16[4,128,1024]{2,1,0:T(8,128)(2,1)} custom-call(bf16[128,1024]{1,0:T(8,128)(2,1)} %convert_element_type.222.refs_0_), custom_call_target="tpu_custom_call" | custom-call | tf_op jit(solution)/shard_map/exchange_5/pallas_call | solution.py:482
  202.6 4.5 %fusion.81 = (f32[1024]{0:T(1024)S(1)}, bf16[512,1024]{1,0:T(8,128)(2,1)S(1)}) fusion(f32[512,1024]{1,0:T(8,128)} %get-tuple-element.353, f32[1024]{0:T(1024)S(1)} %add.153, bf16[512,1024]{1,0:T(8,128)(2,1)} %bitcast.276, bf16[1024,1024]{0,1:T(8,128)(2,1)} %bitcast.268), kind=kOutput, calls=%fused_computation.153 | convolution fusion | flops 1080032256 | bytes 6299648 | tf_op jit(solution)/shard_map/td,fd->tf/dot_general | solution.py:752
  207.2 2.6 convolution_convert_fusion
  209.8 2.7 convolution_convert_fusion.1
  212.4 3.9 copy.68
  217.1 4.2 %convolution_convert_fusion.2 = bf16[512,1024]{1,0:T(8,128)(2,1)} fusion(bf16[1024,1024]{1,0:T(8,128)(2,1)} %bitcast.327, bf16[512,1024]{1,0:T(8,128)(2,1)} %copy-done.28), kind=kOutput, calls=%fused_computation.57 | convolution fusion | flops 1074266112 | bytes 4194304 | tf_op jit(solution)/shard_map/tf,df->td/dot_general | solution.py:757
  221.3 23.8 %exchange_6.1 = (f32[128,1024]{1,0:T(8,128)}, f32[8,1024]{1,0:T(8,128)}, f32[1024,128]{1,0:T(8,128)}) custom-call(bf16[4,128,1024]{2,1,0:T(8,128)(2,1)} %bitcast.273, f32[4,8,1024]{2,1,0:T(8,128)} %broadcast_in_dim.19.refs_1_, bf16[8,1024,128]{2,1,0:T(8,128)(2,1)} %bitcast.258), custom_call_target="tpu_custom_call" | custom-call | tf_op jit(solution)/shard_map/exchange_6/pallas_call | solution.py:482
  245.1 1.3 multiply_reduce_fusion
  248.2 25.2 %exchange_7.1 = (bf16[4,128,1024]{2,1,0:T(8,128)(2,1)}, f32[128,1024]{1,0:T(8,128)}) custom-call(bf16[128,1024]{1,0:T(8,128)(2,1)} %convert_element_type.226.refs_0_, bf16[8,128,1024]{2,1,0:T(8,128)(2,1)} %bitcast.266), custom_call_target="tpu_custom_call" | custom-call | tf_op jit(solution)/shard_map/exchange_7/pallas_call | solution.py:482
  273.4 1.8 convolution_convert_fusion.5
  276.4 1.2 bitcast_reduce_fusion.1
  277.6 50.3 %while.31 = (s32[]{:T(128)}, f32[512,256]{0,1:T(8,128)S(1)}, bf16[4,512,256]{2,1,0:T(8,128)(2,1)}, bf16[4,512,256]{2,1,0:T(8,128)(2,1)}, bf16[4,512,4,64]{1,3,2,...) while((s32[]{:T(128)}, f32[512,256]{0,1:T(8,128)S(1)}, ...), condition=%wide.region_17.18_spmd.clone, body=%wide.region_16.17_spmd.clone.sunk | while | flops 680263680 | bytes 42231960 | solution.py:619
  277.6 1.7 fusion.156
  279.4 2.6 multiply_convert_fusion.3
  282.9 3.1 fusion.157
  286.8 1.8 constant_dynamic-update-slice_fusion.3
  288.6 1.4 convolution_multiply_fusion.3
  290.2 1.7 fusion.156
  291.9 2.6 multiply_convert_fusion.3
  295.5 3.1 fusion.157
  299.4 1.8 constant_dynamic-update-slice_fusion.3
  301.2 1.4 convolution_multiply_fusion.3
  302.8 1.7 fusion.156
  304.5 2.6 multiply_convert_fusion.3
  308.0 3.1 fusion.157
  312.0 1.8 constant_dynamic-update-slice_fusion.3
  313.7 1.4 convolution_multiply_fusion.3
  315.3 1.7 fusion.156
  317.0 2.6 multiply_convert_fusion.3
  320.6 3.1 fusion.157
  324.5 1.8 constant_dynamic-update-slice_fusion.3
  326.3 1.4 convolution_multiply_fusion.3
  327.9 18.6 %exchange_8.1 = (f32[512,256]{1,0:T(8,128)}, f32[512,256]{1,0:T(8,128)}) custom-call(bf16[4,512,256]{2,1,0:T(8,128)(2,1)} %get-tuple-element.151.refs_0_, bf16[4,512,256]{2,1,0:T(8,128)(2,1)} %get-tuple-element.152.refs_1_), custom_call_target="tpu_custom_call" | custom-call | tf_op jit(solution)/shard_map/exchange_8/pallas_call | solution.py:482
  346.5 2.5 convolution_convert_fusion.7
  349.0 1.3 convolution_convert_fusion.6
  352.5 1.5 add_convert_fusion
  354.0 1.3 convolution_convert_fusion.8
  355.3 24.2 %exchange_9.1 = (f32[128,1024]{1,0:T(8,128)}, f32[8,1024]{1,0:T(8,128)}, f32[128,256]{1,0:T(8,128)}, f32[128,256]{1,0:T(8,128)}, f32[128,256]{1,0:T(8,128)}, /*index=5*/f32[256,128]{1,0:T(8,128)}) custom-call(bf16[4,128,1024]{2,1,0:T(8,128)(2,1)} %bitcast.264, f32[4,8,1024]{2,1,0:T(8,128)} %broadcast_in_dim.20.refs_1_, bf16[8,128,256]{2,1,0:T(8,128)(2,1)} %bitcast.271, ...), custom_call_target="tpu_custom_call" | custom-call | tf_op jit(solution)/shard_map/exchange_9/pallas_call | solution.py:482
  382.8 7.8 %exchange_10.1 = f32[8,128]{1,0:T(8,128)} custom-call(f32[8,8,128]{2,1,0:T(8,128)} %bitcast.301), custom_call_target="tpu_custom_call" | custom-call | tf_op jit(solution)/shard_map/exchange_10/pallas_call | solution.py:482
  392.7 1.4 slice_bitcast_fusion.6
  (181 shorter events, 36.9 us)
Async XLA Ops:
  32.3 3.7 copy-start.10
  32.4 3.7 copy-start.20
  54.9 2.4 copy-start.12
  55.0 3.9 copy-start.18
  59.4 31.9 %copy-start.16 = (bf16[8,256,128]{2,1,0:T(8,128)(2,1)S(1)}, bf16[8,256,128]{2,1,0:T(8,128)(2,1)}, u32[]{:S(2)}) copy-start(bf16[8,256,128]{2,1,0:T(8,128)(2,1)} %get-tuple-element.143) | copy-start | bytes 1572868
  63.2 3.5 copy-start
  71.1 3.5 copy-start
  79.0 3.5 copy-start
  87.0 3.5 copy-start
  91.3 27.8 %copy-start.9 = (bf16[1,128,1024]{2,1,0:T(8,128)(2,1)S(1)}, bf16[1,128,1024]{2,1,0:T(8,128)(2,1)}, u32[]{:S(2)}) copy-start(bf16[1,128,1024]{2,1,0:T(8,128)(2,1)} %param.21) | copy-start | bytes 786436
  158.5 21.7 %copy-start.5 = (bf16[1,128,1024]{2,1,0:T(8,128)(2,1)S(1)}, bf16[1,128,1024]{2,1,0:T(8,128)(2,1)}, u32[]{:S(2)}) copy-start(bf16[1,128,1024]{2,1,0:T(8,128)(2,1)} %param.37) | copy-start | bytes 786436
  202.6 4.5 %copy-start.7 = (bf16[4,128,1024]{2,1,0:T(8,128)(2,1)S(1)}, bf16[4,128,1024]{2,1,0:T(8,128)(2,1)}, u32[]{:S(2)}) copy-start(bf16[4,128,1024]{2,1,0:T(8,128)(2,1)} %exchange_3.1) | copy-start | bytes 3145732
  207.1 2.6 copy-start.28
  207.1 2.6 copy-start.8
  207.1 2.6 copy-start.27
  246.6 0.8 copy-start.2
  273.4 3.0 copy-start.4
  279.4 2.7 copy-start.1
  291.9 2.7 copy-start.1
  304.5 2.7 copy-start.1
  317.0 2.7 copy-start.1
  327.9 18.6 %copy-start.11 = (bf16[4,128,1024]{2,1,0:T(8,128)(2,1)S(1)}, bf16[4,128,1024]{2,1,0:T(8,128)(2,1)}, u32[]{:S(2)}) copy-start(bf16[4,128,1024]{2,1,0:T(8,128)(2,1)} %get-tuple-element.134) | copy-start | bytes 3145732
  346.5 2.5 copy-start.6
  346.5 4.5 %copy-start.21 = (bf16[8,128,256]{2,1,0:T(8,128)(2,1)S(1)}, bf16[8,128,256]{2,1,0:T(8,128)(2,1)}, u32[]{:S(2)}) copy-start(bf16[8,128,256]{2,1,0:T(8,128)(2,1)} %get-tuple-element.135) | copy-start | bytes 1572868
  346.5 4.5 %copy-start.22 = (f32[512,256]{1,0:T(8,128)S(1)}, f32[512,256]{1,0:T(8,128)}, u32[]{:S(2)}) copy-start(f32[512,256]{1,0:T(8,128)} %get-tuple-element.153) | copy-start | bytes 1572868
  350.3 1.2 copy-start.19
  351.5 1.0 copy-start.13
  355.3 38.8 %copy-start.3 = (f32[128,1024]{1,0:T(8,128)S(1)}, f32[128,1024]{1,0:T(8,128)}, u32[]{:S(2)}) copy-start(f32[128,1024]{1,0:T(8,128)} %copy-done.2) | copy-start | bytes 1572868
  379.5 14.6 %copy-start.17 = (f32[128,1024]{1,0:T(8,128)S(1)}, f32[128,1024]{1,0:T(8,128)}, u32[]{:S(2)}) copy-start(f32[128,1024]{1,0:T(8,128)} %get-tuple-element.155) | copy-start | bytes 1572868
  379.5 15.4 %copy-start.26 = (f32[128,256]{1,0:T(8,128)S(1)}, f32[128,256]{1,0:T(8,128)}, u32[]{:S(2)}) copy-start(f32[128,256]{1,0:T(8,128)} %get-tuple-element.560) | copy-start | bytes 393220
  379.5 16.1 %copy-start.25 = (f32[128,256]{1,0:T(8,128)S(1)}, f32[128,256]{1,0:T(8,128)}, u32[]{:S(2)}) copy-start(f32[128,256]{1,0:T(8,128)} %get-tuple-element.561) | copy-start | bytes 393220
  379.5 16.7 %copy-start.24 = (f32[128,256]{1,0:T(8,128)S(1)}, f32[128,256]{1,0:T(8,128)}, u32[]{:S(2)}) copy-start(f32[128,256]{1,0:T(8,128)} %get-tuple-element.562) | copy-start | bytes 393220
  379.5 17.3 %copy-start.23 = (f32[256,128]{1,0:T(8,128)S(1)}, f32[256,128]{1,0:T(8,128)}, u32[]{:S(2)}) copy-start(f32[256,128]{1,0:T(8,128)} %get-tuple-element.563) | copy-start | bytes 393220
  380.4 17.1 %copy-start.15 = (f32[128,1024]{1,0:T(8,128)S(1)}, f32[128,1024]{1,0:T(8,128)}, u32[]{:S(2)}) copy-start(f32[128,1024]{1,0:T(8,128)} %get-tuple-element.569) | copy-start | bytes 1572868
  380.8 17.5 %copy-start.14 = (f32[1024,128]{1,0:T(8,128)S(1)}, f32[1024,128]{1,0:T(8,128)}, u32[]{:S(2)}) copy-start(f32[1024,128]{1,0:T(8,128)} %get-tuple-element.571) | copy-start | bytes 1572868

commit v2 on v1

--- a/solution.py
+++ b/solution.py
@@ -121,11 +121,25 @@
     )
 
 
+def slab(slot, width):
+    return pl.ds(pl.multiple_of(slot * width, width), width)
+
+
+def slot_rows(ref, slot, rows, width):
+    return ref.at[slot, rows] if len(ref.shape) == 3 else ref.at[rows, slab(slot, width)]
+
+
 class CubeGather:
-    def __init__(self, axes, arrays):
+    def __init__(self, axes, arrays, columns=(False,) * 8):
         self.axes, self.arrays, self.bits = axes, list(arrays), bits_of(axes)
         self.slots = math.prod(lax.axis_size(name) for name in axes)
-        self.outs = [jax.ShapeDtypeStruct((self.slots,) + a.shape, a.dtype) for a in self.arrays]
+        self.flat = [joined and a.shape[1] % 128 == 0 for a, joined in zip(self.arrays, columns)]
+        self.outs = [
+            jax.ShapeDtypeStruct(
+                (a.shape[0], self.slots * a.shape[1]) if flat else (self.slots,) + a.shape, a.dtype
+            )
+            for a, flat in zip(self.arrays, self.flat)
+        ]
         self.scratch = []
         streams = sum(len(self.parts(a)) for a in self.arrays)
         self.sems = 2 * streams * (self.slots - 1)
@@ -146,7 +160,10 @@
                 gens.append(self.stream(at, me, src, dst, part, order, sems))
         yield from together(gens)
         for src, dst in zip(ins, outs):
-            dst[me] = src[...]
+            if len(dst.shape) == 2:
+                dst[:, slab(me, src.shape[1])] = src[...]
+            else:
+                dst[me] = src[...]
 
     def stream(self, at, me, src, dst, part, order, sems):
         rows = pl.ds(*part)
@@ -157,7 +174,7 @@
                 if sub in landing:
                     landing.pop(sub).wait_recv()
                 slot = flip_all(me, sub)
-                there = dst.at[slot, rows]
+                there = slot_rows(dst, slot, rows, src.shape[1])
                 copy = remote(
                     there if sub else src.at[rows], there, (sems.take(), sems.take()), peer(at, bit)
                 )
@@ -177,21 +194,25 @@
     def __init__(self, axes, arrays):
         self.axes, self.arrays, self.bits = axes, list(arrays), bits_of(axes)
         self.slots = math.prod(lax.axis_size(name) for name in axes)
-        self.outs = [jax.ShapeDtypeStruct(a.shape[1:], jnp.float32) for a in self.arrays]
+        self.outs = [jax.ShapeDtypeStruct(self.piece(a), jnp.float32) for a in self.arrays]
         self.scratch = []
         self.sems = 0
         for a in self.arrays:
+            width = self.piece(a)[1]
             for part in self.parts(a):
                 left = self.slots
                 for unused in self.bits:
                     left //= 2
-                    self.scratch.append(((left, part[1], a.shape[2]), a.dtype))
+                    self.scratch.append(((left, part[1], width), a.dtype))
                     if left > 1:
-                        self.scratch.append(((left, part[1], a.shape[2]), a.dtype))
+                        self.scratch.append(((left, part[1], width), a.dtype))
                 self.sems += 2 * (self.slots - 1)
 
+    def piece(self, array):
+        return array.shape[1:] if array.ndim == 3 else (array.shape[0], array.shape[1] // self.slots)
+
     def parts(self, array):
-        return row_parts(array.shape[1], array.size // self.slots, 16)
+        return row_parts(self.piece(array)[0], array.size // self.slots, 16)
 
     def peers(self, at):
         return [(peer(at, bit), None) for bit in self.bits]
@@ -222,7 +243,7 @@
             copies = []
             for j, sub in enumerate(subs):
                 if level is None:
-                    piece = src.at[flip_all(flip(me, bit[2]), sub), rows]
+                    piece = slot_rows(src, flip_all(flip(me, bit[2]), sub), rows, dst.shape[1])
                 else:
                     piece = level.at[before.index((bit,) + sub)]
                 copy = remote(piece, landed.at[j], (sems.take(), sems.take()), peer(at, bit))
@@ -238,7 +259,12 @@
 
                 def add(here_rows, j=j, slot=slot, old=old, level=level, goal=goal, landed=landed):
                     moved = pl.ds(start + here_rows.start, here_rows.size)
-                    mine = src[slot, moved, :] if level is None else level[old, here_rows, :]
+                    if level is not None:
+                        mine = level[old, here_rows, :]
+                    elif len(src.shape) == 3:
+                        mine = src[slot, moved, :]
+                    else:
+                        mine = src[moved, slab(slot, dst.shape[1])]
                     total = mine.astype(jnp.float32) + landed[j, here_rows, :].astype(jnp.float32)
                     if goal is None:
                         dst[moved, :] = total
@@ -508,7 +534,15 @@
 
 
 def column_slots(grad, slots):
+    if grad.shape[1] % (128 * slots) == 0:
+        return grad.astype(jnp.bfloat16)
     return grad.astype(jnp.bfloat16).reshape(grad.shape[0], slots, -1).transpose(1, 0, 2)
+
+
+def join_columns(gathered):
+    if gathered.ndim == 2:
+        return gathered
+    return gathered.transpose(1, 0, 2).reshape(gathered.shape[1], -1)
 
 
 def spread_rows(vectors, lanes):
@@ -516,130 +550,113 @@
     return jnp.broadcast_to(rows[None], (lanes,) + rows.shape)
 
 
+def contract(left, right, sides):
+    return lax.dot_general(left, right, ((sides[:1], sides[1:]), ((), ())), preferred_element_type=jnp.float32)
+
+
+def heads_at_once(heads_dev):
+    return 2 if heads_dev % 2 == 0 else heads_dev
+
+
 def attend_forward(q_heads, k_all, v_all, heads_dev):
     rows, head_width = q_heads.shape
+    keys = k_all.shape[0]
     scale = DH ** (-0.5)
-    q_three = q_heads.reshape(rows, heads_dev, DH)
-
-    def fold(carry, piece, start):
-        k_piece, v_piece = piece
-        count = k_piece.shape[0]
-        size = math.gcd(count, 512)
-        steps = count // size
-        k_split = k_piece.reshape(steps, size, heads_dev, DH)
-        v_split = v_piece.reshape(steps, size, heads_dev, DH)
-
-        def step(state, blocks):
-            best, total, accum = state
-            k_block, v_block = blocks
-            scores = (
-                jnp.einsum("qhd,khd->hqk", q_three, k_block, preferred_element_type=jnp.float32)
-                * scale
-            )
-            new_best = jnp.maximum(best, jnp.max(scores, axis=-1))
-            fade = jnp.exp(best - new_best)
-            weights = jnp.exp(scores - new_best[:, :, None])
-            total = total * fade + jnp.sum(weights, axis=-1)
-            update = jnp.einsum("hqk,khd->qhd", weights, v_block.astype(jnp.float32))
-            accum = accum.reshape(rows, heads_dev, DH) * fade.T[:, :, None] + update
-            return ((new_best, total, accum.reshape(rows, head_width)), None)
-
-        state, unused = lax.scan(step, carry, (k_split, v_split))
-        return state
-
-    start_state = (
-        jnp.full((heads_dev, rows), -jnp.inf, jnp.float32),
-        jnp.zeros((heads_dev, rows), jnp.float32),
-        jnp.zeros((rows, head_width), jnp.float32),
-    )
-    best, total, accum = fold(
-        start_state,
-        (
-            k_all,
-            v_all,
-        ),
-        jnp.int32(0),
-    )
-    attended = (accum.reshape(rows, heads_dev, DH) / total.T[:, :, None]).reshape(rows, head_width)
-    return (attended.astype(jnp.bfloat16), best + jnp.log(total))
+    pair = heads_at_once(heads_dev)
+    wide = pair * DH
+    step = math.gcd(rows, 256)
+
+    def kernel(q_ref, k_ref, v_ref, out_ref, lse_ref):
+        for block in range(rows // step):
+            here_rows = slice(block * step, (block + 1) * step)
+            sums = []
+            for h in range(pair):
+                cols = slice(h * DH, (h + 1) * DH)
+                scores = contract(k_ref[:, cols], q_ref[here_rows, cols], (1, 1)) * scale
+                best = jnp.max(scores, axis=0, keepdims=True)
+                weights = jnp.exp(scores - best)
+                total = jnp.sum(weights, axis=0, keepdims=True)
+                accum = contract(v_ref[:, cols], weights.astype(jnp.bfloat16), (0, 0))
+                sums.append(accum / total)
+                lse_ref[0, h : h + 1, here_rows] = best + jnp.log(total)
+            out_ref[here_rows, :] = jnp.concatenate(sums, axis=0).T.astype(jnp.bfloat16)
+
+    return pl.pallas_call(
+        kernel,
+        name="attend_forward",
+        grid=(heads_dev // pair,),
+        in_specs=[
+            pl.BlockSpec((rows, wide), lambda g: (0, g)),
+            pl.BlockSpec((keys, wide), lambda g: (0, g)),
+            pl.BlockSpec((keys, wide), lambda g: (0, g)),
+        ],
+        out_specs=[
+            pl.BlockSpec((rows, wide), lambda g: (0, g)),
+            pl.BlockSpec((1, pair, rows), lambda g: (g, 0, 0)),
+        ],
+        out_shape=[
+            jax.ShapeDtypeStruct((rows, head_width), jnp.bfloat16),
+            jax.ShapeDtypeStruct((heads_dev // pair, pair, rows), jnp.float32),
+        ],
+    )(q_heads, k_all, v_all)
 
 
 def attend_backward(q_heads, k_all, v_all, attended, lse, d_att, heads_dev):
     rows, head_width = q_heads.shape
+    keys = k_all.shape[0]
     scale = DH ** (-0.5)
-    q_three = q_heads.reshape(rows, heads_dev, DH)
-    do_three = d_att.reshape(rows, heads_dev, DH)
-    delta = (
-        (d_att.astype(jnp.float32) * attended.astype(jnp.float32))
-        .reshape(rows, heads_dev, DH)
-        .sum(-1)
-        .T
-    )
-    all_keys = rows * lax.axis_size("blk")
-
-    def fold(carry, piece, start):
-        dq_accum, key_accum = carry
-        k_piece, v_piece = piece
-        count = k_piece.shape[0]
-        size = math.gcd(count, 512)
-        steps = count // size
-        k_split = k_piece.reshape(steps, size, heads_dev, DH)
-        v_split = v_piece.reshape(steps, size, heads_dev, DH)
-
-        def step(dq_state, blocks):
-            k_block, v_block = blocks
-            scores = (
-                jnp.einsum("qhd,khd->hqk", q_three, k_block, preferred_element_type=jnp.float32)
-                * scale
-            )
-            weights = jnp.exp(scores - lse[:, :, None])
-            weights_round = weights.astype(jnp.bfloat16)
-            v_part = jnp.einsum(
-                "hqk,qhd->khd", weights_round, do_three, preferred_element_type=jnp.float32
-            )
-            d_weights = jnp.einsum(
-                "qhd,khd->hqk", do_three, v_block, preferred_element_type=jnp.float32
-            )
-            d_scores = (weights * (d_weights - delta[:, :, None])).astype(jnp.bfloat16)
-            q_part = (
-                jnp.einsum("hqk,khd->qhd", d_scores, k_block, preferred_element_type=jnp.float32)
-                * scale
-            )
-            k_part = (
-                jnp.einsum("hqk,qhd->khd", d_scores, q_three, preferred_element_type=jnp.float32)
-                * scale
-            )
-            dq_state = dq_state + q_part.reshape(rows, head_width)
-            both = (
-                k_part.reshape(size, head_width).astype(jnp.bfloat16),
-                v_part.reshape(size, head_width).astype(jnp.bfloat16),
-            )
-            return (dq_state, both)
-
-        dq_accum, parts = lax.scan(step, dq_accum, (k_split, v_split))
-        return (dq_accum, parts)
-
-    start_state = (
-        jnp.zeros((rows, head_width), jnp.float32),
-        None,
-    )
-    dq_accum, key_accum = fold(
-        start_state,
-        (
-            k_all,
-            v_all,
-        ),
-        jnp.int32(0),
-    )
-    blocks = lax.axis_size("blk")
-    owned = communicate(
-        8, [CubeScatter(("blk",), [part.reshape(blocks, rows, head_width) for part in key_accum])]
-    )[0]
-    return (
-        dq_accum.astype(jnp.bfloat16),
-        owned[0].astype(jnp.bfloat16),
-        owned[1].astype(jnp.bfloat16),
-    )
+    pair = heads_at_once(heads_dev)
+    wide = pair * DH
+    size = math.gcd(keys, 512)
+    steps = keys // size
+
+    def kernel(q_ref, k_ref, v_ref, att_ref, lse_ref, d_ref, dq_ref, dk_ref, dv_ref, accum, delta):
+        step = pl.program_id(1)
+
+        @pl.when(step == 0)
+        def unused_start():
+            accum[...] = jnp.zeros_like(accum)
+            both = (d_ref[...].astype(jnp.float32) * att_ref[...].astype(jnp.float32)).T
+            for h in range(pair):
+                delta[h : h + 1, :] = jnp.sum(both[h * DH : (h + 1) * DH], axis=0, keepdims=True)
+
+        for h in range(pair):
+            cols = slice(h * DH, (h + 1) * DH)
+            k_head, q_head, d_head = k_ref[:, cols], q_ref[:, cols], d_ref[:, cols]
+            scores = contract(k_head, q_head, (1, 1)) * scale
+            weights = jnp.exp(scores - lse_ref[0, h : h + 1, :])
+            d_weights = contract(v_ref[:, cols], d_head, (1, 1))
+            d_scores = (weights * (d_weights - delta[h : h + 1, :])).astype(jnp.bfloat16)
+            dv_ref[:, cols] = contract(weights.astype(jnp.bfloat16), d_head, (1, 0)).astype(jnp.bfloat16)
+            dk_ref[:, cols] = (contract(d_scores, q_head, (1, 0)) * scale).astype(jnp.bfloat16)
+            accum[cols, :] += contract(k_head, d_scores, (0, 0))
+
+        @pl.when(step == steps - 1)
+        def unused_end():
+            dq_ref[...] = (accum[...] * scale).T.astype(jnp.bfloat16)
+
+    across = pl.BlockSpec((rows, wide), lambda g, s: (0, g))
+    down = pl.BlockSpec((size, wide), lambda g, s: (s, g))
+    return pl.pallas_call(
+        kernel,
+        name="attend_backward",
+        grid=(heads_dev // pair, steps),
+        in_specs=[
+            across,
+            down,
+            down,
+            across,
+            pl.BlockSpec((1, pair, rows), lambda g, s: (g, 0, 0)),
+            across,
+        ],
+        out_specs=[across, down, down],
+        out_shape=[
+            jax.ShapeDtypeStruct((rows, head_width), jnp.bfloat16),
+            jax.ShapeDtypeStruct((keys, head_width), jnp.bfloat16),
+            jax.ShapeDtypeStruct((keys, head_width), jnp.bfloat16),
+        ],
+        scratch_shapes=[pltpu.VMEM((wide, rows), jnp.float32), pltpu.VMEM((pair, rows), jnp.float32)],
+    )(q_heads, k_all, v_all, attended, lse, d_att)
 
 
 def local(
@@ -694,12 +711,13 @@
                     out_weight,
                     pack([a.reshape(1, -1) for a in small_in], 1)[0],
                 ],
+                (False, False, False, True, False),
             ),
         ],
     )
     rows_all = tok_all.reshape(-1, width)
     w_query, w_key, w_value = (w.reshape(width, head_width) for w in (q3, k3, v3))
-    w_out = o3.transpose(1, 0, 2).reshape(head_width, width)
+    w_out = join_columns(o3)
     flat = small.reshape(slots, -1)
     vectors = []
     start = 0
@@ -721,11 +739,11 @@
         2,
         [
             LineScatter([mat(attended, w_out).astype(jnp.bfloat16).reshape(lanes, tok_rows, width)]),
-            CubeGather(group, [inner_weight, outer_weight]),
+            CubeGather(group, [inner_weight, outer_weight], (False, True)),
         ],
     )
     w_inner = inner3.reshape(width, inner_width)
-    w_outer = outer3.transpose(1, 0, 2).reshape(inner_width, width)
+    w_outer = join_columns(outer3)
     resid_one = rows_in.astype(jnp.float32) + attn_sum + b_out
     normed_one, unit_one, rstd_one = norm_forward(
         resid_one, gain_one, shift_one
@@ -777,23 +795,35 @@
     d_att = jnp.einsum("td,ed->te", d_one_all, w_out, preferred_element_type=jnp.float32).astype(
         jnp.bfloat16
     )
-    dq_heads, dk_heads, dv_heads = attend_backward(
+    dq_heads, k_terms, v_terms = attend_backward(
         q_heads, k_all, v_all, attended, lse, d_att, heads_dev
     )
+    extras_one = spread_rows([g_gain_one, g_shift_one, g_out_b], lanes)
+    (sums_one,), owned = communicate(
+        8,
+        [
+            LineScatter([extras_one]),
+            CubeScatter(("blk",), [part.reshape(blocks, -1, head_width) for part in (k_terms, v_terms)]),
+        ],
+    )
+    dk_heads, dv_heads = (part.astype(jnp.bfloat16) for part in owned)
     g_query_w = jnp.einsum("td,te->de", rows_all, dq_heads, preferred_element_type=jnp.float32)
     g_key_w = jnp.einsum("td,te->de", rows_all, dk_heads, preferred_element_type=jnp.float32)
     g_value_w = jnp.einsum("td,te->de", rows_all, dv_heads, preferred_element_type=jnp.float32)
     g_query_b = jnp.sum(dq_heads.astype(jnp.float32), axis=0).reshape(-1, DH)
     g_value_b = jnp.sum(dv_heads.astype(jnp.float32), axis=0).reshape(-1, DH)
-    extras_one = spread_rows([g_gain_one, g_shift_one, g_out_b], lanes)
+    small_out = [v.reshape(slots, -1) for v in (*sums_one[:3], *sums_two[:3])]
+    for bias in (g_query_b, g_value_b, g_inner_b):
+        count = bias.shape[0]
+        small_out.append(bias.reshape(count, slots, -1).transpose(1, 0, 2).reshape(slots, -1))
     back = None
     for grad, weight in ((dq_heads, w_query), (dk_heads, w_key), (dv_heads, w_value)):
         term = jnp.einsum("te,de->td", grad, weight, preferred_element_type=jnp.float32)
         back = term if back is None else back + term
-    (back_sum, sums_one), (r_query, r_key, r_value, r_out) = communicate(
+    (back_sum,), (r_query, r_key, r_value, r_out, kept) = communicate(
         9,
         [
-            LineScatter([back.astype(jnp.bfloat16).reshape(lanes, tok_rows, width), extras_one]),
+            LineScatter([back.astype(jnp.bfloat16).reshape(lanes, tok_rows, width)]),
             CubeScatter(
                 group,
                 [
@@ -801,16 +831,13 @@
                     row_slots(g_key_w, slots),
                     row_slots(g_value_w, slots),
                     column_slots(g_out_w, slots),
+                    pack(small_out, slots),
                 ],
             ),
         ],
     )
     tokens_grad = (d_resid_one + back_sum).astype(jnp.bfloat16)[None]
-    small_out = [v.reshape(slots, -1) for v in (*sums_one[:3], *sums_two[:3])]
-    for bias in (g_query_b, g_value_b, g_inner_b):
-        count = bias.shape[0]
-        small_out.append(bias.reshape(count, slots, -1).transpose(1, 0, 2).reshape(slots, -1))
-    kept = communicate(10, [CubeScatter(group, [pack(small_out, slots)])])[0][0].reshape(-1)
+    kept = kept.reshape(-1)
     ends = []
     start = 0
     for piece in small_out:

time: 403 us -> 327 us (0.81)
  matrix products: 105 us -> 38.7 us
  local copies, waits for them, and re-layouts: 43 us -> 19.6 us
  Pallas kernels: 236 us -> 254 us
    dot_general x28 -> x0, matrix products: 66.2 us -> none  [the longest x8 21.4 us: step(): jnp.einsum('qhd,khd->hqk', q_three, k_block, preferred_element_type=jnp.f...]
    pallas_call x0 -> x2, Pallas kernels: none -> 27.2 us  [the longest x1 14.8 us: attend_backward(): pl.pallas_call(kernel, name='attend_backward', grid=(heads_dev // pair, s...]
    dynamic_update_slice x12 -> x0, local copies, waits for them, and re-layouts: 11.1 us -> none  [fold(): dq_accum, parts = lax.scan(step, dq_accum, (k_split, v_split))]
    pallas_call x11 -> x10, Pallas kernels: 236 us -> 227 us  [communicate(): pl.pallas_call(kernel, name='exchange_%d' % number, out_shape=outs, in_sp...]
    reshape x2 -> x0, local copies, waits for them, and re-layouts: 4.94 us -> none  [column_slots(): grad.astype(jnp.bfloat16).reshape(grad.shape[0], slots, -1)]
    transpose x2 -> x0, local copies, waits for them, and re-layouts: 4.14 us -> none  [the longest x1 3.93 us: local(): w_outer = outer3.transpose(1, 0, 2).reshape(inner_width, width)]
    unnamed x65 -> x61, local copies, waits for them, and re-layouts: 8.57 us -> 9.98 us
where the time goes in v2:
time: 327 us; the launch traced here: 325 us
  Pallas kernels  254 us (78%)
  matrix products  38.7 us (12%)
  local copies, waits for them, and re-layouts  19.6 us (6%)
  other arithmetic  11 us (3%)
    pallas_call x10, Pallas kernels, communicate(): pl.pallas_call(kernel, name='exchange_%d' % number, out_shape=outs, in_sp...  227 us
    pallas_call x1, Pallas kernels, attend_backward(): pl.pallas_call(kernel, name='attend_backward', grid=(heads_dev // pair, s...  14.8 us
    dot_general x6, matrix products, mat(): return jnp.dot(left, right, preferred_element_type=jnp.float32)  14.2 us
    pallas_call x1, Pallas kernels, attend_forward(): pl.pallas_call(kernel, name='attend_forward', grid=(heads_dev // pair,),...  12.4 us
    unnamed x61, local copies, waits for them, and re-layouts  9.98 us

profile of v2, /device:TPU:0, one launch (start us, length us, event | category | flops | bytes accessed | tf_op | source)
XLA Modules:
  0.0 324.8 jit_solution(12715602379989380922)
XLA Ops:
  0.7 0.8 convert_element_type.158
  1.4 0.8 convert_element_type.159
  2.2 0.8 copy.42
  2.9 0.1 convert_element_type.160
  3.0 0.8 concatenate.7
  3.9 0.6 pad_convert_fusion
  4.5 27.9 %exchange_0.1 = (bf16[4,128,1024]{2,1,0:T(8,128)(2,1)}, bf16[8,128,256]{2,1,0:T(8,128)(2,1)}, bf16[8,128,256]{2,1,0:T(8,128)(2,1)}, bf16[8,128,256]{2,1,0:T(8,12...) custom-call(bf16[128,1024]{1,0:T(8,128)(2,1)} %bitcast.156, bf16[128,256]{1,0:T(8,128)(2,1)} %refs_1_.2, ...), custom_call_target="tpu_custom_call" | custom-call | tf_op jit(solution)/shard_map/exchange_0/pallas_call | solution.py:508
  32.4 0.9 copy.57
  33.8 2.5 fusion.5.q_ref
  36.3 1.1 convolution_convert_fusion.10.refs_0_
  37.7 1.1 fusion.6.refs_1_
  38.8 17.8 %exchange_1.1 = (bf16[4,512,256]{2,1,0:T(8,128)(2,1)}, bf16[4,512,256]{2,1,0:T(8,128)(2,1)}) custom-call(bf16[512,256]{1,0:T(8,128)(2,1)} %convolution_convert_fusion.10.refs_0_, bf16[512,256]{1,0:T(8,128)(2,1)} %fusion.6.refs_1_), custom_call_target="tpu_custom_call" | custom-call | tf_op jit(solution)/shard_map/exchange_1/pallas_call | solution.py:508
  56.7 12.4 %attend_forward.1 = (bf16[512,256]{1,0:T(8,128)(2,1)}, f32[2,2,512]{2,1,0:T(2,128)}) custom-call(bf16[512,256]{1,0:T(8,128)(2,1)} %fusion.5.q_ref, bf16[2048,256]{1,0:T(8,128)(2,1)} %bitcast.144, bf16[2048,256]{1,0:T(8,128)(2,1)} %bitcast.146), custom_call_target="tpu_custom_call" | custom-call | tf_op jit(solution)/shard_map/attend_forward/pallas_call | solution.py:584
  69.1 2.4 convolution_convert_fusion.4
  71.5 26.0 %exchange_2.1 = (f32[128,1024]{1,0:T(8,128)}, bf16[8,128,1024]{2,1,0:T(8,128)(2,1)}, bf16[1024,1024]{1,0:T(8,128)(2,1)}) custom-call(bf16[4,128,1024]{2,1,0:T(8,128)(2,1)} %bitcast.142, bf16[128,1024]{1,0:T(8,128)(2,1)} %refs_1_.3, bf16[1024,128]{1,0:T(8,128)(2,1)} %refs_2_.3), custom_call_target="tpu_custom_call" | custom-call | tf_op jit(solution)/shard_map/exchange_2/pallas_call | solution.py:508
  97.5 1.2 fusion.30
  98.7 0.2 multiply_reduce_fusion.3
  98.9 0.9 fusion.18.refs_0_
  99.8 23.8 %exchange_3.1 = bf16[4,128,1024]{2,1,0:T(8,128)(2,1)} custom-call(bf16[128,1024]{1,0:T(8,128)(2,1)} %fusion.18.refs_0_), custom_call_target="tpu_custom_call" | custom-call | tf_op jit(solution)/shard_map/exchange_3/pallas_call | solution.py:508
  123.6 4.8 %multiply_convert_fusion = (bf16[512,1024]{1,0:T(8,128)(2,1)S(1)}, f32[512,1024]{1,0:T(8,128)}) fusion(f32[1024]{0:T(1024)S(1)} %add.135, bf16[512,1024]{1,0:T(8,128)(2,1)} %bitcast.150, bf16[1024,1024]{1,0:T(8,128)(2,1)} %bitcast.198), kind=kOutput, calls=%fused_computation.7 | convolution fusion | flops 1076887552 | bytes 6295552 | tf_op jit(solution)/shard_map/dot_general | solution.py:40
  128.3 2.2 convolution_convert_fusion.3
  130.6 20.1 %exchange_4.1 = f32[128,1024]{1,0:T(8,128)} custom-call(bf16[4,128,1024]{2,1,0:T(8,128)(2,1)} %bitcast.157), custom_call_target="tpu_custom_call" | custom-call | tf_op jit(solution)/shard_map/exchange_4/pallas_call | solution.py:508
  150.7 1.3 fusion.29
  152.0 0.2 multiply_reduce_fusion.2
  152.2 0.3 fusion.15
  152.5 1.0 fusion.27
  153.5 0.7 convert_element_type.171.refs_0_
  154.2 20.4 %exchange_5.1 = bf16[4,128,1024]{2,1,0:T(8,128)(2,1)} custom-call(bf16[128,1024]{1,0:T(8,128)(2,1)} %convert_element_type.171.refs_0_), custom_call_target="tpu_custom_call" | custom-call | tf_op jit(solution)/shard_map/exchange_5/pallas_call | solution.py:508
  174.7 4.6 %fusion.35 = (f32[1024]{0:T(1024)S(1)}, bf16[512,1024]{1,0:T(8,128)(2,1)S(1)}) fusion(f32[512,1024]{1,0:T(8,128)} %get-tuple-element.152, f32[1024]{0:T(1024)S(1)} %add.135, bf16[512,1024]{1,0:T(8,128)(2,1)} %bitcast.154, bf16[1024,1024]{1,0:T(8,128)(2,1)} %get-tuple-element.58), kind=kOutput, calls=%fused_computation.99 | convolution fusion | flops 1080032256 | bytes 6299648 | tf_op jit(solution)/shard_map/td,fd->tf/dot_general | solution.py:770
  179.3 2.3 convolution_convert_fusion.2
  181.7 0.7 broadcast_in_dim.9.refs_1_
  182.3 2.7 convolution_convert_fusion.1.refs_2_
  185.0 23.8 %exchange_6.1 = (f32[128,1024]{1,0:T(8,128)}, f32[8,1024]{1,0:T(8,128)}, f32[1024,128]{1,0:T(8,128)}) custom-call(bf16[4,128,1024]{2,1,0:T(8,128)(2,1)} %bitcast.149, f32[4,8,1024]{2,1,0:T(8,128)} %broadcast_in_dim.9.refs_1_, bf16[1024,1024]{1,0:T(8,128)(2,1)} %convolution_convert_fusion.1.refs_2_), custom_call_target="tpu_custom_call" | custom-call | tf_op jit(solution)/shard_map/exchange_6/pallas_call | solution.py:508
  208.8 1.5 multiply_reduce_fusion
  210.3 0.2 fusion.26
  210.5 0.7 convert_element_type.175.refs_0_
  211.2 2.6 convolution_convert_fusion
  213.9 24.9 %exchange_7.1 = (bf16[4,128,1024]{2,1,0:T(8,128)(2,1)}, f32[128,1024]{1,0:T(8,128)}) custom-call(bf16[128,1024]{1,0:T(8,128)(2,1)} %convert_element_type.175.refs_0_, bf16[8,128,1024]{2,1,0:T(8,128)(2,1)} %bitcast.148), custom_call_target="tpu_custom_call" | custom-call | tf_op jit(solution)/shard_map/exchange_7/pallas_call | solution.py:508
  238.8 2.4 convolution_convert_fusion.9.d_ref
  241.2 14.8 %attend_backward.1 = (bf16[512,256]{1,0:T(8,128)(2,1)}, bf16[2048,256]{1,0:T(8,128)(2,1)}, bf16[2048,256]{1,0:T(8,128)(2,1)}) custom-call(bf16[512,256]{1,0:T(8,128)(2,1)} %fusion.5.q_ref, bf16[2048,256]{1,0:T(8,128)(2,1)} %bitcast.145, bf16[2048,256]{1,0:T(8,128)(2,1)} %bitcast.147, bf16[512,256]{1,0:T(8,128)(2,1)} %get-tuple-element.54.att_ref, ...), custom_call_target="tpu_custom_call" | custom-call | tf_op jit(solution)/shard_map/attend_backward/pallas_call | solution.py:640
  256.0 1.4 fusion.36
  257.5 0.7 broadcast_in_dim.10.refs_0_
  258.1 19.0 %exchange_8.1 = (f32[8,1024]{1,0:T(8,128)}, f32[512,256]{1,0:T(8,128)}, f32[512,256]{1,0:T(8,128)}) custom-call(f32[4,8,1024]{2,1,0:T(8,128)} %broadcast_in_dim.10.refs_0_, bf16[4,512,256]{2,1,0:T(8,128)(2,1)} %bitcast.158, bf16[4,512,256]{2,1,0:T(8,128)(2,1)} %bitcast.159), custom_call_target="tpu_custom_call" | custom-call | tf_op jit(solution)/shard_map/exchange_8/pallas_call | solution.py:508
  277.2 1.8 fusion.22
  279.0 1.6 add_convert_fusion
  280.6 1.3 convolution_convert_fusion.8
  281.9 1.3 convolution_convert_fusion.7
  283.2 1.3 convolution_convert_fusion.6
  284.5 1.3 convolution_convert_fusion.5.refs_4_
  285.8 0.9 fusion.33
  286.7 0.9 fusion.32
  288.4 0.6 copy.56
  289.0 23.5 %exchange_9.1 = (f32[128,1024]{1,0:T(8,128)}, f32[128,256]{1,0:T(8,128)}, f32[128,256]{1,0:T(8,128)}, f32[128,256]{1,0:T(8,128)}, f32[256,128]{1,0:T(8,128)}, /*index=5*/f32[8,128]{1,0:T(8,128)}) custom-call(bf16[4,128,1024]{2,1,0:T(8,128)(2,1)} %bitcast.143, bf16[8,128,256]{2,1,0:T(8,128)(2,1)} %bitcast.162, bf16[8,128,256]{2,1,0:T(8,128)(2,1)} %bitcast.163, ...), custom_call_target="tpu_custom_call" | custom-call | tf_op jit(solution)/shard_map/exchange_9/pallas_call | solution.py:508
  312.5 1.9 fusion.20
  314.4 0.8 slice.94
  315.1 0.6 fusion.31
  315.7 1.4 slice_bitcast_fusion.6
  317.2 0.7 copy.49
  317.8 1.6 copy.66
  319.4 1.6 copy.67
  321.0 1.6 copy.68
  322.5 0.7 copy.69
  323.2 0.8 copy.70
  324.0 0.8 copy.71
  (85 shorter events, 1.7 us)
Async XLA Ops:
  32.4 4.0 %copy-start.13 = (bf16[8,128,256]{2,1,0:T(8,128)(2,1)S(1)}, bf16[8,128,256]{2,1,0:T(8,128)(2,1)}, u32[]{:S(2)}) copy-start(bf16[8,128,256]{2,1,0:T(8,128)(2,1)} %get-tuple-element.50) | copy-start | bytes 1572868
  32.4 3.9 %copy-start.19 = (bf16[4,128,1024]{2,1,0:T(8,128)(2,1)S(1)}, bf16[4,128,1024]{2,1,0:T(8,128)(2,1)}, u32[]{:S(2)}) copy-start(bf16[4,128,1024]{2,1,0:T(8,128)(2,1)} %get-tuple-element.47) | copy-start | bytes 3145732
  33.5 4.2 %copy-start.8 = (bf16[8,128,256]{2,1,0:T(8,128)(2,1)S(1)}, bf16[8,128,256]{2,1,0:T(8,128)(2,1)}, u32[]{:S(2)}) copy-start(bf16[8,128,256]{2,1,0:T(8,128)(2,1)} %get-tuple-element.51) | copy-start | bytes 1572868
  37.7 31.4 %copy-start.10 = (bf16[256,1024]{1,0:T(8,128)(2,1)S(1)}, bf16[256,1024]{1,0:T(8,128)(2,1)}, u32[]{:S(2)}) copy-start(bf16[256,1024]{1,0:T(8,128)(2,1)} %get-tuple-element.55) | copy-start | bytes 1572868
  69.1 28.4 %copy-start.6 = (bf16[1,128,1024]{2,1,0:T(8,128)(2,1)S(1)}, bf16[1,128,1024]{2,1,0:T(8,128)(2,1)}, u32[]{:S(2)}) copy-start(bf16[1,128,1024]{2,1,0:T(8,128)(2,1)} %param.17) | copy-start | bytes 786436
  123.5 4.8 %copy-start.18 = (bf16[1024,1024]{1,0:T(8,128)(2,1)S(1)}, bf16[1024,1024]{1,0:T(8,128)(2,1)}, u32[]{:S(2)}) copy-start(bf16[1024,1024]{1,0:T(8,128)(2,1)} %get-tuple-element.58) | copy-start | bytes 6291460
  128.3 2.2 copy-start.21
  130.5 21.7 %copy-start = (bf16[1,128,1024]{2,1,0:T(8,128)(2,1)S(1)}, bf16[1,128,1024]{2,1,0:T(8,128)(2,1)}, u32[]{:S(2)}) copy-start(bf16[1,128,1024]{2,1,0:T(8,128)(2,1)} %param.33) | copy-start | bytes 786436
  174.7 4.6 %copy-start.17 = (bf16[8,128,1024]{2,1,0:T(8,128)(2,1)S(1)}, bf16[8,128,1024]{2,1,0:T(8,128)(2,1)}, u32[]{:S(2)}) copy-start(bf16[8,128,1024]{2,1,0:T(8,128)(2,1)} %get-tuple-element.57) | copy-start | bytes 6291460
  179.3 2.3 copy-start.23
  179.3 3.0 copy-start.5
  179.3 3.0 copy-start.22
  208.8 2.5 copy-start.3
  208.8 2.5 copy-start.24
  241.2 14.8 %copy-start.14 = (bf16[8,128,256]{2,1,0:T(8,128)(2,1)S(1)}, bf16[8,128,256]{2,1,0:T(8,128)(2,1)}, u32[]{:S(2)}) copy-start(bf16[8,128,256]{2,1,0:T(8,128)(2,1)} %get-tuple-element.48) | copy-start | bytes 1572868
  277.2 1.8 copy-start.2
  277.2 1.8 copy-start.9
  279.0 1.6 copy-start.7
  279.0 1.6 copy-start.20
  280.6 1.3 copy-start.15
  281.9 2.6 copy-start.1
  281.9 2.6 copy-start.4
  289.0 34.2 %copy-start.12 = (f32[128,1024]{1,0:T(8,128)S(1)}, f32[128,1024]{1,0:T(8,128)}, u32[]{:S(2)}) copy-start(f32[128,1024]{1,0:T(8,128)} %get-tuple-element.187) | copy-start | bytes 1572868
  312.5 10.0 %copy-start.16 = (f32[256,128]{1,0:T(8,128)S(1)}, f32[256,128]{1,0:T(8,128)}, u32[]{:S(2)}) copy-start(f32[256,128]{1,0:T(8,128)} %get-tuple-element.181) | copy-start | bytes 393220
  312.5 11.5 %copy-start.11 = (f32[1024,128]{1,0:T(8,128)S(1)}, f32[1024,128]{1,0:T(8,128)}, u32[]{:S(2)}) copy-start(f32[1024,128]{1,0:T(8,128)} %get-tuple-element.189) | copy-start | bytes 1572868

commit v3 on v2

--- a/solution.py
+++ b/solution.py
@@ -554,108 +554,213 @@
     return lax.dot_general(left, right, ((sides[:1], sides[1:]), ((), ())), preferred_element_type=jnp.float32)
 
 
-def heads_at_once(heads_dev):
-    return 2 if heads_dev % 2 == 0 else heads_dev
-
-
-def attend_forward(q_heads, k_all, v_all, heads_dev):
+def greet(at, bits):
+    barrier = pltpu.get_barrier_semaphore()
+    for bit in bits:
+        pl.semaphore_signal(barrier, inc=1, device_id=peer(at, bit), device_id_type=MESH)
+    pl.semaphore_wait(barrier, len(bits))
+
+
+def attend_forward(q_heads, k_heads, v_heads, heads_dev):
     rows, head_width = q_heads.shape
-    keys = k_all.shape[0]
     scale = DH ** (-0.5)
-    pair = heads_at_once(heads_dev)
-    wide = pair * DH
+    bits = bits_of(("blk",))
+    blocks = lax.axis_size("blk")
+    order = bits[1:] + bits[:1]
+    subs = sorted(subsets(order)[1:], key=lambda sub: (sub != tuple(bits[:1]), len(sub)))
     step = math.gcd(rows, 256)
 
-    def kernel(q_ref, k_ref, v_ref, out_ref, lse_ref):
-        for block in range(rows // step):
-            here_rows = slice(block * step, (block + 1) * step)
-            sums = []
-            for h in range(pair):
-                cols = slice(h * DH, (h + 1) * DH)
-                scores = contract(k_ref[:, cols], q_ref[here_rows, cols], (1, 1)) * scale
-                best = jnp.max(scores, axis=0, keepdims=True)
-                weights = jnp.exp(scores - best)
-                total = jnp.sum(weights, axis=0, keepdims=True)
-                accum = contract(v_ref[:, cols], weights.astype(jnp.bfloat16), (0, 0))
-                sums.append(accum / total)
-                lse_ref[0, h : h + 1, here_rows] = best + jnp.log(total)
-            out_ref[here_rows, :] = jnp.concatenate(sums, axis=0).T.astype(jnp.bfloat16)
-
+    def kernel(q_ref, k_ref, v_ref, k_all, v_all, out_ref, lse_ref, best, total, accum, sem_ref):
+        at = here()
+        me = at["blk"]
+        greet(at, bits)
+        sems = Sems(sem_ref)
+        landing, sent = {}, []
+
+        def pass_on(sub):
+            first = order.index(sub[-1]) + 1 if sub else 0
+            slot = flip_all(me, sub)
+            for bit in order[first:]:
+                copies = []
+                for src, dst in ((k_ref, k_all), (v_ref, v_all)):
+                    piece = dst.at[slot] if sub else src
+                    copies.append(
+                        remote(piece, dst.at[slot], (sems.take(), sems.take()), peer(at, bit))
+                    )
+                    copies[-1].start()
+                landing[sub + (bit,)] = copies
+                sent.extend(copies)
+
+        def fold(k_piece, v_piece, slot):
+            def turn(i, carry):
+                span = pl.ds(pl.multiple_of(i * step, step), step)
+                for h in range(heads_dev):
+                    cols = slice(h * DH, (h + 1) * DH)
+                    one = slice(h, h + 1)
+                    k_head = k_piece[:, cols] if slot is None else k_piece[slot, :, cols]
+                    v_head = v_piece[:, cols] if slot is None else v_piece[slot, :, cols]
+                    scores = contract(k_head, q_ref[span, cols], (1, 1)) * scale
+                    top = jnp.max(scores, axis=0, keepdims=True)
+                    if slot is not None:
+                        top = jnp.maximum(best[one, span], top)
+                    weights = jnp.exp(scores - top)
+                    mass = jnp.sum(weights, axis=0, keepdims=True)
+                    update = contract(v_head, weights.astype(jnp.bfloat16), (0, 0))
+                    if slot is not None:
+                        fade = jnp.exp(best[one, span] - top)
+                        mass = mass + total[one, span] * fade
+                        update = update + accum[cols, span] * fade
+                    best[one, span] = top
+                    total[one, span] = mass
+                    accum[cols, span] = update
+                return carry
+
+            lax.fori_loop(0, rows // step, turn, 0)
+
+        pass_on(())
+        fold(k_ref, v_ref, None)
+        for sub in subs:
+            for copy in landing[sub]:
+                copy.wait_recv()
+            pass_on(sub)
+            fold(k_all, v_all, flip_all(me, sub))
+        k_all[me] = k_ref[...]
+        v_all[me] = v_ref[...]
+        lse_ref[...] = best[...] + jnp.log(total[...])
+        for h in range(heads_dev):
+            cols = slice(h * DH, (h + 1) * DH)
+            accum[cols, :] = accum[cols, :] / total[h : h + 1, :]
+        out_ref[...] = accum[...].T.astype(jnp.bfloat16)
+        for copy in sent:
+            copy.wait_send()
+
+    vmem = pl.BlockSpec(memory_space=pltpu.VMEM)
+    whole = jax.ShapeDtypeStruct((blocks, rows, head_width), jnp.bfloat16)
     return pl.pallas_call(
         kernel,
         name="attend_forward",
-        grid=(heads_dev // pair,),
-        in_specs=[
-            pl.BlockSpec((rows, wide), lambda g: (0, g)),
-            pl.BlockSpec((keys, wide), lambda g: (0, g)),
-            pl.BlockSpec((keys, wide), lambda g: (0, g)),
+        in_specs=[vmem] * 3,
+        out_specs=[vmem] * 4,
+        out_shape=[
+            whole,
+            whole,
+            jax.ShapeDtypeStruct((rows, head_width), jnp.bfloat16),
+            jax.ShapeDtypeStruct((heads_dev, rows), jnp.float32),
         ],
-        out_specs=[
-            pl.BlockSpec((rows, wide), lambda g: (0, g)),
-            pl.BlockSpec((1, pair, rows), lambda g: (g, 0, 0)),
+        scratch_shapes=[
+            pltpu.VMEM((heads_dev, rows), jnp.float32),
+            pltpu.VMEM((heads_dev, rows), jnp.float32),
+            pltpu.VMEM((head_width, rows), jnp.float32),
+            pltpu.SemaphoreType.DMA((4 * (blocks - 1),)),
         ],
-        out_shape=[
-            jax.ShapeDtypeStruct((rows, head_width), jnp.bfloat16),
-            jax.ShapeDtypeStruct((heads_dev // pair, pair, rows), jnp.float32),
-        ],
-    )(q_heads, k_all, v_all)
+        compiler_params=pltpu.CompilerParams(collective_id=1, has_side_effects=True),
+    )(q_heads, k_heads, v_heads)
 
 
 def attend_backward(q_heads, k_all, v_all, attended, lse, d_att, heads_dev):
     rows, head_width = q_heads.shape
-    keys = k_all.shape[0]
+    blocks = lax.axis_size("blk")
     scale = DH ** (-0.5)
-    pair = heads_at_once(heads_dev)
-    wide = pair * DH
-    size = math.gcd(keys, 512)
-    steps = keys // size
-
-    def kernel(q_ref, k_ref, v_ref, att_ref, lse_ref, d_ref, dq_ref, dk_ref, dv_ref, accum, delta):
-        step = pl.program_id(1)
-
-        @pl.when(step == 0)
-        def unused_start():
-            accum[...] = jnp.zeros_like(accum)
-            both = (d_ref[...].astype(jnp.float32) * att_ref[...].astype(jnp.float32)).T
-            for h in range(pair):
-                delta[h : h + 1, :] = jnp.sum(both[h * DH : (h + 1) * DH], axis=0, keepdims=True)
-
-        for h in range(pair):
-            cols = slice(h * DH, (h + 1) * DH)
-            k_head, q_head, d_head = k_ref[:, cols], q_ref[:, cols], d_ref[:, cols]
-            scores = contract(k_head, q_head, (1, 1)) * scale
-            weights = jnp.exp(scores - lse_ref[0, h : h + 1, :])
-            d_weights = contract(v_ref[:, cols], d_head, (1, 1))
-            d_scores = (weights * (d_weights - delta[h : h + 1, :])).astype(jnp.bfloat16)
-            dv_ref[:, cols] = contract(weights.astype(jnp.bfloat16), d_head, (1, 0)).astype(jnp.bfloat16)
-            dk_ref[:, cols] = (contract(d_scores, q_head, (1, 0)) * scale).astype(jnp.bfloat16)
-            accum[cols, :] += contract(k_head, d_scores, (0, 0))
-
-        @pl.when(step == steps - 1)
-        def unused_end():
-            dq_ref[...] = (accum[...] * scale).T.astype(jnp.bfloat16)
-
-    across = pl.BlockSpec((rows, wide), lambda g, s: (0, g))
-    down = pl.BlockSpec((size, wide), lambda g, s: (s, g))
+    bits = bits_of(("blk",))
+    core, far = tuple(bits[:1]), bits[1:]
+    fars = sorted(subsets(far), key=lambda sub: [bit not in sub for bit in far])
+    size = math.gcd(rows, 256)
+
+    def kernel(
+        q_ref, k_ref, v_ref, att_ref, lse_ref, d_ref, dq_ref, dk_ref, dv_ref,
+        accum, delta, given, kept, landed, summed, arrived, sem_ref,
+    ):
+        at = here()
+        me = at["blk"]
+        greet(at, bits)
+        sems = Sems(sem_ref)
+        accum[...] = jnp.zeros_like(accum)
+        both = (d_ref[...].astype(jnp.float32) * att_ref[...].astype(jnp.float32)).T
+        for h in range(heads_dev):
+            delta[h : h + 1, :] = jnp.sum(both[h * DH : (h + 1) * DH], axis=0, keepdims=True)
+
+        def terms(slot, goal, index):
+            def turn(i, carry):
+                span = pl.ds(pl.multiple_of(i * size, size), size)
+                for h in range(heads_dev):
+                    cols = slice(h * DH, (h + 1) * DH)
+                    one = slice(h, h + 1)
+                    k_head, q_head, d_head = k_ref[slot, span, cols], q_ref[:, cols], d_ref[:, cols]
+                    scores = contract(k_head, q_head, (1, 1)) * scale
+                    weights = jnp.exp(scores - lse_ref[one, :])
+                    d_weights = contract(v_ref[slot, span, cols], d_head, (1, 1))
+                    d_scores = (weights * (d_weights - delta[one, :])).astype(jnp.bfloat16)
+                    v_part = contract(weights.astype(jnp.bfloat16), d_head, (1, 0))
+                    k_part = contract(d_scores, q_head, (1, 0)) * scale
+                    goal[index, 0, span, cols] = k_part.astype(jnp.bfloat16)
+                    goal[index, 1, span, cols] = v_part.astype(jnp.bfloat16)
+                    accum[cols, :] += contract(k_head, d_scores, (0, 0))
+                return carry
+
+            lax.fori_loop(0, rows // size, turn, 0)
+
+        sent, coming = [], {}
+        for index, sub in enumerate(fars):
+            terms(flip_all(me, sub + core), given, index)
+            copy = remote(
+                given.at[index], landed.at[index], (sems.take(), sems.take()), peer(at, core[0])
+            )
+            copy.start()
+            sent.append(copy)
+            terms(flip_all(me, sub), kept, index)
+            sources = [(landed, index)]
+            copy.wait_recv()
+            link = None
+            for bit in far:
+                if bit in sub:
+                    link = bit
+                    break
+                other = coming[(bit, sub)]
+                other[0].wait_recv()
+                sources.append((arrived, other[1]))
+
+            def add(span, index=index, sources=sources, link=link):
+                for which, result in ((0, dk_ref), (1, dv_ref)):
+                    value = kept[index, which, span, :].astype(jnp.float32)
+                    for ref, place in sources:
+                        value = value + ref[place, which, span, :].astype(jnp.float32)
+                    if link is None:
+                        result[span, :] = value.astype(jnp.bfloat16)
+                    else:
+                        summed[index, which, span, :] = value.astype(jnp.bfloat16)
+
+            row_loop(rows, add)
+            if link is not None:
+                copy = remote(
+                    summed.at[index], arrived.at[index], (sems.take(), sems.take()), peer(at, link)
+                )
+                copy.start()
+                sent.append(copy)
+                coming[(link, tuple(bit for bit in sub if bit != link))] = (copy, index)
+        dq_ref[...] = (accum[...] * scale).T.astype(jnp.bfloat16)
+        for copy in sent:
+            copy.wait_send()
+
+    vmem = pl.BlockSpec(memory_space=pltpu.VMEM)
+    out = jax.ShapeDtypeStruct((rows, head_width), jnp.bfloat16)
+    room = pltpu.VMEM((len(fars), 2, rows, head_width), jnp.bfloat16)
     return pl.pallas_call(
         kernel,
         name="attend_backward",
-        grid=(heads_dev // pair, steps),
-        in_specs=[
-            across,
-            down,
-            down,
-            across,
-            pl.BlockSpec((1, pair, rows), lambda g, s: (g, 0, 0)),
-            across,
+        in_specs=[vmem] * 6,
+        out_specs=[vmem] * 3,
+        out_shape=[out, out, out],
+        scratch_shapes=[
+            pltpu.VMEM((head_width, rows), jnp.float32),
+            pltpu.VMEM((heads_dev, rows), jnp.float32),
+            room,
+            room,
+            room,
+            room,
+            room,
+            pltpu.SemaphoreType.DMA((4 * len(fars) - 2,)),
         ],
-        out_specs=[across, down, down],
-        out_shape=[
-            jax.ShapeDtypeStruct((rows, head_width), jnp.bfloat16),
-            jax.ShapeDtypeStruct((keys, head_width), jnp.bfloat16),
-            jax.ShapeDtypeStruct((keys, head_width), jnp.bfloat16),
-        ],
-        scratch_shapes=[pltpu.VMEM((wide, rows), jnp.float32), pltpu.VMEM((pair, rows), jnp.float32)],
+        compiler_params=pltpu.CompilerParams(collective_id=8, has_side_effects=True),
     )(q_heads, k_all, v_all, attended, lse, d_att)
 
 
@@ -680,7 +785,6 @@
 ):
     group = ("dp", "blk")
     slots = lax.axis_size("dp") * lax.axis_size("blk")
-    blocks = lax.axis_size("blk")
     lanes = lax.axis_size("ulysses")
     rows_in = tokens[0]
     tok_rows, width = rows_in.shape
@@ -731,25 +835,25 @@
     q_heads = (mat(rows_all, w_query) + b_query).astype(jnp.bfloat16)
     k_heads = mat(rows_all, w_key).astype(jnp.bfloat16)
     v_heads = (mat(rows_all, w_value) + b_value).astype(jnp.bfloat16)
-    k_all, v_all = communicate(1, [CubeGather(("blk",), [k_heads, v_heads])])[0]
-    k_all = k_all.reshape(-1, head_width)
-    v_all = v_all.reshape(-1, head_width)
-    attended, lse = attend_forward(q_heads, k_all, v_all, heads_dev)
-    (attn_sum,), (inner3, outer3) = communicate(
+    k_all, v_all, attended, lse = attend_forward(q_heads, k_heads, v_heads, heads_dev)
+    (attn_sum,), (inner3,) = communicate(
         2,
         [
             LineScatter([mat(attended, w_out).astype(jnp.bfloat16).reshape(lanes, tok_rows, width)]),
-            CubeGather(group, [inner_weight, outer_weight], (False, True)),
+            CubeGather(group, [inner_weight]),
         ],
     )
     w_inner = inner3.reshape(width, inner_width)
-    w_outer = join_columns(outer3)
     resid_one = rows_in.astype(jnp.float32) + attn_sum + b_out
     normed_one, unit_one, rstd_one = norm_forward(
         resid_one, gain_one, shift_one
     )
     normed_round = normed_one.astype(jnp.bfloat16)
-    normed_all = communicate(3, [LineGather([normed_round])])[0][0].reshape(-1, width)
+    (normed_all,), (outer3,) = communicate(
+        3, [LineGather([normed_round]), CubeGather(group, [outer_weight], (True,))]
+    )
+    normed_all = normed_all.reshape(-1, width)
+    w_outer = join_columns(outer3)
     pre_act = mat(normed_all, w_inner) + b_inner
     act_full, slope = gelu_parts(pre_act)
     activation = act_full.astype(jnp.bfloat16)
@@ -786,27 +890,23 @@
     )
     g_out_b = jnp.sum(d_resid_one, axis=0)
     d_one_round = d_resid_one.astype(jnp.bfloat16)
-    (d_one_all,), (r_inner,) = communicate(
+    extras_one = spread_rows([g_gain_one, g_shift_one, g_out_b], lanes)
+    (d_one_all,), (sums_one,), (r_inner,) = communicate(
         7,
-        [LineGather([d_one_round]), CubeScatter(group, [row_slots(g_inner_w, slots)])],
+        [
+            LineGather([d_one_round]),
+            LineScatter([extras_one]),
+            CubeScatter(group, [row_slots(g_inner_w, slots)]),
+        ],
     )
     d_one_all = d_one_all.reshape(-1, width)
     g_out_w = jnp.einsum("te,td->ed", attended, d_one_all, preferred_element_type=jnp.float32)
     d_att = jnp.einsum("td,ed->te", d_one_all, w_out, preferred_element_type=jnp.float32).astype(
         jnp.bfloat16
     )
-    dq_heads, k_terms, v_terms = attend_backward(
+    dq_heads, dk_heads, dv_heads = attend_backward(
         q_heads, k_all, v_all, attended, lse, d_att, heads_dev
     )
-    extras_one = spread_rows([g_gain_one, g_shift_one, g_out_b], lanes)
-    (sums_one,), owned = communicate(
-        8,
-        [
-            LineScatter([extras_one]),
-            CubeScatter(("blk",), [part.reshape(blocks, -1, head_width) for part in (k_terms, v_terms)]),
-        ],
-    )
-    dk_heads, dv_heads = (part.astype(jnp.bfloat16) for part in owned)
     g_query_w = jnp.einsum("td,te->de", rows_all, dq_heads, preferred_element_type=jnp.float32)
     g_key_w = jnp.einsum("td,te->de", rows_all, dk_heads, preferred_element_type=jnp.float32)
     g_value_w = jnp.einsum("td,te->de", rows_all, dv_heads, preferred_element_type=jnp.float32)

time: 327 us -> 307 us (0.939)
  Pallas kernels: 254 us -> 233 us
    pallas_call x10 -> x8, Pallas kernels: 227 us -> 186 us  [communicate(): pl.pallas_call(kernel, name='exchange_%d' % number, out_shape=outs, in_sp...]
    pallas_call x2, Pallas kernels: 27.2 us -> 46.9 us  [the longest x1 24.1 us: attend_forward(): pl.pallas_call(kernel, name='attend_forward', in_specs=[vmem] * 3, out_sp...]
    unnamed x61 -> x55, local copies, waits for them, and re-layouts: 9.98 us -> 10.4 us
where the time goes in v3:
time: 307 us; the launch traced here: 304 us
  Pallas kernels  233 us (76%)
  matrix products  36.3 us (12%)
  local copies, waits for them, and re-layouts  20.1 us (7%)
  other arithmetic  12.8 us (4%)
    pallas_call x8, Pallas kernels, communicate(): pl.pallas_call(kernel, name='exchange_%d' % number, out_shape=outs, in_sp...  186 us
    pallas_call x1, Pallas kernels, attend_forward(): pl.pallas_call(kernel, name='attend_forward', in_specs=[vmem] * 3, out_sp...  24.1 us
    pallas_call x1, Pallas kernels, attend_backward(): pl.pallas_call(kernel, name='attend_backward', in_specs=[vmem] * 6, out_s...  22.8 us
    dot_general x6, matrix products, mat(): return jnp.dot(left, right, preferred_element_type=jnp.float32)  14.2 us
    unnamed x55, local copies, waits for them, and re-layouts  10.4 us

profile of v3, /device:TPU:0, one launch (start us, length us, event | category | flops | bytes accessed | tf_op | source)
XLA Modules:
  0.0 303.5 jit_solution(14242249396006837423)
XLA Ops:
  0.7 0.8 copy.42
  1.5 0.8 convert_element_type.152
  2.3 0.8 convert_element_type.153
  3.0 0.8 concatenate.7
  3.9 0.6 pad_convert_fusion
  4.5 27.8 %exchange_0.1 = (bf16[4,128,1024]{2,1,0:T(8,128)(2,1)}, bf16[8,128,256]{2,1,0:T(8,128)(2,1)}, bf16[8,128,256]{2,1,0:T(8,128)(2,1)}, bf16[8,128,256]{2,1,0:T(8,12...) custom-call(bf16[128,1024]{1,0:T(8,128)(2,1)} %bitcast.150, bf16[128,256]{1,0:T(8,128)(2,1)} %refs_1_.3, ...), custom_call_target="tpu_custom_call" | custom-call | tf_op jit(solution)/shard_map/exchange_0/pallas_call | solution.py:508
  32.3 0.9 copy.57
  33.5 2.6 fusion.5.q_ref
  36.2 1.1 fusion.6.v_ref
  37.4 1.1 convolution_convert_fusion.10.k_ref
  38.5 24.1 %attend_forward.1 = (bf16[4,512,256]{2,1,0:T(8,128)(2,1)}, bf16[4,512,256]{2,1,0:T(8,128)(2,1)}, bf16[512,256]{1,0:T(8,128)(2,1)}, f32[4,512]{1,0:T(4,128)}) custom-call(bf16[512,256]{1,0:T(8,128)(2,1)} %fusion.5.q_ref, bf16[512,256]{1,0:T(8,128)(2,1)} %convolution_convert_fusion.10.k_ref, bf16[512,256]{1,0:T(8,128)(2,1)} %fusion.6.v_ref), custom_call_target="tpu_custom_call" | custom-call | tf_op jit(solution)/shard_map/attend_forward/pallas_call | solution.py:639
  62.6 2.4 convolution_convert_fusion.4
  65.0 22.7 %exchange_2.1 = (f32[128,1024]{1,0:T(8,128)}, bf16[8,128,1024]{2,1,0:T(8,128)(2,1)}) custom-call(bf16[4,128,1024]{2,1,0:T(8,128)(2,1)} %bitcast.142, bf16[128,1024]{1,0:T(8,128)(2,1)} %refs_1_.4), custom_call_target="tpu_custom_call" | custom-call | tf_op jit(solution)/shard_map/exchange_2/pallas_call | solution.py:508
  87.8 1.2 fusion.25
  89.0 0.2 multiply_reduce_fusion.3
  89.2 0.9 fusion.18.refs_0_
  90.1 22.9 %exchange_3.1 = (bf16[4,128,1024]{2,1,0:T(8,128)(2,1)}, bf16[1024,1024]{1,0:T(8,128)(2,1)}) custom-call(bf16[128,1024]{1,0:T(8,128)(2,1)} %fusion.18.refs_0_, bf16[1024,128]{1,0:T(8,128)(2,1)} %refs_1_.5), custom_call_target="tpu_custom_call" | custom-call | tf_op jit(solution)/shard_map/exchange_3/pallas_call | solution.py:508
  113.2 4.8 %multiply_convert_fusion = (bf16[512,1024]{1,0:T(8,128)(2,1)S(1)}, f32[512,1024]{1,0:T(8,128)}) fusion(f32[1024]{0:T(1024)S(1)} %add.135, bf16[512,1024]{1,0:T(8,128)(2,1)} %bitcast.198, bf16[1024,1024]{1,0:T(8,128)(2,1)} %bitcast.190), kind=kOutput, calls=%fused_computation.7 | convolution fusion | flops 1076887552 | bytes 6295552 | tf_op jit(solution)/shard_map/dot_general | solution.py:40
  118.0 2.2 convolution_convert_fusion.3
  120.2 20.2 %exchange_4.1 = f32[128,1024]{1,0:T(8,128)} custom-call(bf16[4,128,1024]{2,1,0:T(8,128)(2,1)} %bitcast.151), custom_call_target="tpu_custom_call" | custom-call | tf_op jit(solution)/shard_map/exchange_4/pallas_call | solution.py:508
  140.4 1.3 fusion.24
  141.8 0.2 multiply_reduce_fusion.2
  142.0 0.3 fusion.15
  142.3 1.0 fusion.22
  143.2 0.7 convert_element_type.165.refs_0_
  144.0 19.4 %exchange_5.1 = bf16[4,128,1024]{2,1,0:T(8,128)(2,1)} custom-call(bf16[128,1024]{1,0:T(8,128)(2,1)} %convert_element_type.165.refs_0_), custom_call_target="tpu_custom_call" | custom-call | tf_op jit(solution)/shard_map/exchange_5/pallas_call | solution.py:508
  163.4 4.5 %fusion.30 = (f32[1024]{0:T(1024)S(1)}, bf16[512,1024]{1,0:T(8,128)(2,1)S(1)}) fusion(f32[512,1024]{1,0:T(8,128)} %get-tuple-element.150, f32[1024]{0:T(1024)S(1)} %add.135, bf16[512,1024]{1,0:T(8,128)(2,1)} %bitcast.148, bf16[1024,1024]{1,0:T(8,128)(2,1)} %get-tuple-element.56), kind=kOutput, calls=%fused_computation.94 | convolution fusion | flops 1080032256 | bytes 6299648 | tf_op jit(solution)/shard_map/td,fd->tf/dot_general | solution.py:874
  167.9 2.6 convolution_convert_fusion
  170.5 2.6 convolution_convert_fusion.1.refs_2_
  173.2 0.7 broadcast_in_dim.9.refs_1_
  173.9 2.3 convolution_convert_fusion.2
  176.2 24.9 %exchange_6.1 = (f32[128,1024]{1,0:T(8,128)}, f32[8,1024]{1,0:T(8,128)}, f32[1024,128]{1,0:T(8,128)}) custom-call(bf16[4,128,1024]{2,1,0:T(8,128)(2,1)} %bitcast.145, f32[4,8,1024]{2,1,0:T(8,128)} %broadcast_in_dim.9.refs_1_, bf16[1024,1024]{1,0:T(8,128)(2,1)} %convolution_convert_fusion.1.refs_2_), custom_call_target="tpu_custom_call" | custom-call | tf_op jit(solution)/shard_map/exchange_6/pallas_call | solution.py:508
  201.1 1.4 multiply_reduce_fusion
  202.5 0.2 fusion.21
  202.7 0.7 broadcast_in_dim.10.refs_1_
  203.4 0.7 convert_element_type.169.refs_0_
  204.1 25.2 %exchange_7.1 = (bf16[4,128,1024]{2,1,0:T(8,128)(2,1)}, f32[8,1024]{1,0:T(8,128)}, f32[128,1024]{1,0:T(8,128)}) custom-call(bf16[128,1024]{1,0:T(8,128)(2,1)} %convert_element_type.169.refs_0_, f32[4,8,1024]{2,1,0:T(8,128)} %broadcast_in_dim.10.refs_1_, bf16[8,128,1024]{2,1,0:T(8,128)(2,1)} %bitcast.144), custom_call_target="tpu_custom_call" | custom-call | tf_op jit(solution)/shard_map/exchange_7/pallas_call | solution.py:508
  229.3 2.4 convolution_convert_fusion.9.d_ref
  231.7 22.8 %attend_backward.1 = (bf16[512,256]{1,0:T(8,128)(2,1)}, bf16[512,256]{1,0:T(8,128)(2,1)}, bf16[512,256]{1,0:T(8,128)(2,1)}) custom-call(bf16[512,256]{1,0:T(8,128)(2,1)} %fusion.5.q_ref, bf16[4,512,256]{2,1,0:T(8,128)(2,1)} %get-tuple-element.58.k_ref, bf16[4,512,256]{2,1,0:T(8,128)(2,1)} %get-tuple-element.59.v_ref, ...), custom_call_target="tpu_custom_call" | custom-call | tf_op jit(solution)/shard_map/attend_backward/pallas_call | solution.py:747
  254.5 1.1 convert_reduce_fusion.2
  255.8 1.0 convert_reduce_fusion.1
  257.0 0.9 fusion.28
  257.9 0.9 fusion.27
  259.1 0.6 copy.56
  259.7 1.3 convolution_convert_fusion.5.refs_4_
  261.0 0.5 fusion.32
  261.5 0.5 fusion.31
  262.0 0.5 copy-done.5
  262.4 1.5 add_convert_fusion
  263.9 1.3 convolution_convert_fusion.8
  265.2 1.3 convolution_convert_fusion.7
  266.5 1.3 convolution_convert_fusion.6
  267.8 23.3 %exchange_9.1 = (f32[128,1024]{1,0:T(8,128)}, f32[128,256]{1,0:T(8,128)}, f32[128,256]{1,0:T(8,128)}, f32[128,256]{1,0:T(8,128)}, f32[256,128]{1,0:T(8,128)}, /*index=5*/f32[8,128]{1,0:T(8,128)}) custom-call(bf16[4,128,1024]{2,1,0:T(8,128)(2,1)} %bitcast.143, bf16[8,128,256]{2,1,0:T(8,128)(2,1)} %bitcast.154, bf16[8,128,256]{2,1,0:T(8,128)(2,1)} %bitcast.155, ...), custom_call_target="tpu_custom_call" | custom-call | tf_op jit(solution)/shard_map/exchange_9/pallas_call | solution.py:508
  291.2 1.9 fusion.20
  293.1 0.8 slice.94
  293.9 0.7 copy.49
  294.5 0.6 fusion.26
  295.1 1.4 slice_bitcast_fusion.6
  296.6 1.6 copy.66
  298.1 1.6 copy.67
  299.7 1.6 copy.68
  301.3 0.7 copy.69
  301.9 0.8 copy.70
  302.7 0.8 copy.71
  (77 shorter events, 1.6 us)
Async XLA Ops:
  32.3 3.9 %copy-start.7 = (bf16[8,128,256]{2,1,0:T(8,128)(2,1)S(1)}, bf16[8,128,256]{2,1,0:T(8,128)(2,1)}, u32[]{:S(2)}) copy-start(bf16[8,128,256]{2,1,0:T(8,128)(2,1)} %get-tuple-element.50) | copy-start | bytes 1572868
  32.3 3.9 %copy-start.17 = (bf16[4,128,1024]{2,1,0:T(8,128)(2,1)S(1)}, bf16[4,128,1024]{2,1,0:T(8,128)(2,1)}, u32[]{:S(2)}) copy-start(bf16[4,128,1024]{2,1,0:T(8,128)(2,1)} %get-tuple-element.46) | copy-start | bytes 3145732
  33.4 4.0 %copy-start.12 = (bf16[8,128,256]{2,1,0:T(8,128)(2,1)S(1)}, bf16[8,128,256]{2,1,0:T(8,128)(2,1)}, u32[]{:S(2)}) copy-start(bf16[8,128,256]{2,1,0:T(8,128)(2,1)} %get-tuple-element.49) | copy-start | bytes 1572868
  36.2 26.4 %copy-start.8 = (bf16[256,1024]{1,0:T(8,128)(2,1)S(1)}, bf16[256,1024]{1,0:T(8,128)(2,1)}, u32[]{:S(2)}) copy-start(bf16[256,1024]{1,0:T(8,128)(2,1)} %get-tuple-element.52) | copy-start | bytes 1572868
  38.5 49.3 %copy-start.4 = (bf16[1,128,1024]{2,1,0:T(8,128)(2,1)S(1)}, bf16[1,128,1024]{2,1,0:T(8,128)(2,1)}, u32[]{:S(2)}) copy-start(bf16[1,128,1024]{2,1,0:T(8,128)(2,1)} %param.17) | copy-start | bytes 786436
  113.2 4.8 %copy-start.16 = (bf16[1024,1024]{1,0:T(8,128)(2,1)S(1)}, bf16[1024,1024]{1,0:T(8,128)(2,1)}, u32[]{:S(2)}) copy-start(bf16[1024,1024]{1,0:T(8,128)(2,1)} %get-tuple-element.56) | copy-start | bytes 6291460
  118.0 2.2 copy-start.20
  120.2 21.7 %copy-start = (bf16[1,128,1024]{2,1,0:T(8,128)(2,1)S(1)}, bf16[1,128,1024]{2,1,0:T(8,128)(2,1)}, u32[]{:S(2)}) copy-start(bf16[1,128,1024]{2,1,0:T(8,128)(2,1)} %param.33) | copy-start | bytes 786436
  163.4 4.5 %copy-start.19 = (bf16[4,128,1024]{2,1,0:T(8,128)(2,1)S(1)}, bf16[4,128,1024]{2,1,0:T(8,128)(2,1)}, u32[]{:S(2)}) copy-start(bf16[4,128,1024]{2,1,0:T(8,128)(2,1)} %get-tuple-element.54) | copy-start | bytes 3145732
  167.9 2.6 copy-start.3
  167.9 2.6 copy-start.21
  170.5 3.4 %copy-start.15 = (bf16[8,128,1024]{2,1,0:T(8,128)(2,1)S(1)}, bf16[8,128,1024]{2,1,0:T(8,128)(2,1)}, u32[]{:S(2)}) copy-start(bf16[8,128,1024]{2,1,0:T(8,128)(2,1)} %get-tuple-element.55) | copy-start | bytes 6291460
  231.7 28.0 %copy-start.1 = (bf16[512,256]{1,0:T(8,128)(2,1)S(1)}, bf16[512,256]{1,0:T(8,128)(2,1)}, u32[]{:S(2)}) copy-start(bf16[512,256]{1,0:T(8,128)(2,1)} %get-tuple-element.51.att_ref) | copy-start | bytes 786436
  231.7 28.0 %copy-start.2 = (bf16[4,128,1024]{2,1,0:T(8,128)(2,1)S(1)}, bf16[4,128,1024]{2,1,0:T(8,128)(2,1)}, u32[]{:S(2)}) copy-start(bf16[4,128,1024]{2,1,0:T(8,128)(2,1)} %get-tuple-element.61) | copy-start | bytes 3145732
  254.5 6.5 %copy-start.13 = (bf16[512,256]{1,0:T(8,128)(2,1)S(1)}, bf16[512,256]{1,0:T(8,128)(2,1)}, u32[]{:S(2)}) copy-start(bf16[512,256]{1,0:T(8,128)(2,1)} %get-tuple-element.63) | copy-start | bytes 786436
  259.7 1.8 copy-start.6
  259.7 1.8 copy-start.11
  261.5 1.0 copy-start.5
  262.4 1.5 copy-start.18
  267.8 34.1 %copy-start.10 = (f32[128,1024]{1,0:T(8,128)S(1)}, f32[128,1024]{1,0:T(8,128)}, u32[]{:S(2)}) copy-start(f32[128,1024]{1,0:T(8,128)} %get-tuple-element.185) | copy-start | bytes 1572868
  291.2 10.1 %copy-start.14 = (f32[256,128]{1,0:T(8,128)S(1)}, f32[256,128]{1,0:T(8,128)}, u32[]{:S(2)}) copy-start(f32[256,128]{1,0:T(8,128)} %get-tuple-element.179) | copy-start | bytes 393220
  291.2 11.5 %copy-start.9 = (f32[1024,128]{1,0:T(8,128)S(1)}, f32[1024,128]{1,0:T(8,128)}, u32[]{:S(2)}) copy-start(f32[1024,128]{1,0:T(8,128)} %get-tuple-element.187) | copy-start | bytes 1572868
